TPU v7x, 128 devices: a whole 4x4x4 slice. The times are simulated.
128 devices in a mesh: photo: 8 (over y, x_lo), tile: 16 (over x_hi, z, core).
Axes of the slice: x: 4 (x_hi: 2, x_lo: 2; x = x_hi * 2 + x_lo), y: 4, z: 4, core: 2. Of those that a mesh axis runs over, the one named last changes fastest.
Arguments:
- photos: bfloat16 [128, 256, 4096], P('photo', 'tile'), may hold values from 0.25 to 64, as said below
- camera_id: int32 [128], P('photo'), may hold values from 0 to 31, never falling along the last dimension, each value on 1 to 8 neighbouring positions
Outputs:
- fingerprints: float32 [32, 256, 4096], P(None, 'tile', 'photo')
- correlation: float32 [32, 32], replicated
Inputs may be any that keep to these rules, and one draw needn't show every extreme that they name: `photos`: values are positive intensities. `camera_id`: photos are ordered by camera: ids never fall, every camera has 1 to 8 photos, and one has exactly 8.
All inputs are finite; a program needn't handle non-finite values.
Results may differ from a plain program's by a relative error of at most 0.0026.
Values may be sent and summed in bfloat16 or wider, within the bound.
A program may use at most 192 MiB of HBM per device.

v0:
```python
import jax
import jax.numpy as jnp
from jax import lax
from jax.sharding import PartitionSpec as P

CAMS = 32


noise_power = 1.0
var_eps = 1e-06


def extended(shard, sides, width):
    for axis, dim in sides:
        size, length = (lax.axis_size(axis), shard.shape[dim])
        up = [(i, (i + 1) % size) for i in range(size - 1)]
        down = [(j, i) for i, j in up]
        last = lax.slice_in_dim(shard, length - width, length, axis=dim)
        leading = lax.slice_in_dim(shard, 0, width, axis=dim)
        before = lax.ppermute(last, axis, up)
        after = lax.ppermute(leading, axis, down)
        shard = jnp.concatenate([before, shard, after], axis=dim)
    return shard


def forward_haar(field):
    top_left = field[..., 0::2, 0::2]
    top_right = field[..., 0::2, 1::2]
    low_left = field[..., 1::2, 0::2]
    low_right = field[..., 1::2, 1::2]
    horiz = (top_left + top_right - low_left - low_right) * 0.5
    vertic = (top_left - top_right + low_left - low_right) * 0.5
    diagon = (top_left - top_right - low_left + low_right) * 0.5
    return jnp.stack([horiz, vertic, diagon])


def inverse_haar(bands):
    horiz, vertic, diagon = (bands[0], bands[1], bands[2])
    top_left = (horiz + vertic + diagon) * 0.5
    top_right = (horiz - vertic - diagon) * 0.5
    low_left = (vertic - horiz - diagon) * 0.5
    low_right = (diagon - horiz - vertic) * 0.5
    upper = jnp.stack([top_left, top_right], -1).reshape(top_left.shape[:-1] + (-1,))
    lower = jnp.stack([low_left, low_right], -1).reshape(low_left.shape[:-1] + (-1,))
    joined = jnp.stack([upper, lower], -2)
    return joined.reshape(upper.shape[:-2] + (-1, upper.shape[-1]))


def local_variance(padded, rows, cols):
    squares = padded * padded
    column_box = squares[..., :, 4 : 4 + cols]
    lowest = None
    for radius in range(1, 5):
        column_box = (
            column_box
            + squares[..., :, 4 - radius : 4 - radius + cols]
            + squares[..., :, 4 + radius : 4 + radius + cols]
        )
        row_box = column_box[..., 4 : 4 + rows, :]
        for offset in range(1, radius + 1):
            row_box = (
                row_box
                + column_box[..., 4 - offset : 4 - offset + rows, :]
                + column_box[..., 4 + offset : 4 + offset + rows, :]
            )
        mean_square = row_box / float((2 * radius + 1) ** 2)
        lowest = mean_square if lowest is None else jnp.minimum(lowest, mean_square)
    return lowest


def camera_totals(selector, noise_part, image_part):
    field = image_part.astype(jnp.float32)
    product = noise_part.astype(jnp.float32) * field
    weighted_part = jnp.einsum(
        "cp,prw->crw",
        selector,
        product,
        precision=lax.Precision.HIGHEST,
        preferred_element_type=jnp.float32,
    )
    energy_part = jnp.einsum(
        "cp,prw->crw",
        selector,
        field * field,
        precision=lax.Precision.HIGHEST,
        preferred_element_type=jnp.float32,
    )
    return (weighted_part, energy_part)


def on_device(photos, camera_id):
    tile_rows = photos.shape[1]
    width_all = photos.shape[2]
    half_rows = tile_rows // 2
    half_cols = width_all // 2
    bands_own = forward_haar(photos.astype(jnp.float32))
    bands_ext = extended(bands_own, (("tile", 2),), 4)
    centre = bands_ext[:, :, 4 : 4 + half_rows, :]
    padded = jnp.pad(bands_ext, ((0, 0), (0, 0), (0, 0), (4, 4)))
    variance = local_variance(padded, half_rows, half_cols)
    gain = noise_power / jnp.maximum(variance, noise_power)
    noise_map = inverse_haar(centre * gain).astype(jnp.bfloat16)
    cameras = jnp.arange(CAMS, dtype=jnp.int32)
    groups = lax.axis_size("photo")
    block = width_all // groups
    selector = (cameras[:, None] == camera_id[None, :]).astype(jnp.float32)
    weighted_part, energy_part = camera_totals(selector, noise_map, photos)
    stacked = jnp.stack([weighted_part, energy_part])
    stacked = stacked.reshape(2, CAMS, tile_rows, 1 * lax.axis_size("photo"), block)
    owned = lax.psum_scatter(
        jnp.transpose(stacked, (3, 0, 1, 2, 4)), "photo", scatter_dimension=0, tiled=True
    )
    weighted = owned[0, 0]
    energy = owned[0, 1]
    fingerprints = weighted / energy
    flat = fingerprints.reshape(CAMS, -1)
    gram_local = jnp.dot(
        flat, flat.T, precision=lax.Precision.HIGHEST, preferred_element_type=jnp.float32
    )
    totals_local = jnp.sum(flat, axis=1)
    gram, totals = lax.psum((gram_local, totals_local), ("photo", "tile"))
    pixel_count = float(tile_rows * lax.axis_size("tile") * width_all)
    average = totals / pixel_count
    covar = gram / pixel_count - average[:, None] * average[None, :]
    spread = jnp.diagonal(covar) + var_eps
    correlation = covar / jnp.sqrt(spread[:, None] * spread[None, :])
    return (fingerprints, correlation)


def solution(mesh):
    placed = (P("photo", "tile", None), P("photo"))
    return jax.shard_map(
        on_device,
        mesh=mesh,
        in_specs=placed,
        out_specs=(P(None, "tile", "photo"), P()),
        check_vma=False,
    )
```

profile of v0, /device:TPU:1, one launch (start us, length us, event | category | flops | bytes accessed | tf_op | source)
XLA Modules:
  0.0 752.6 jit_solution(5499501981493276759)
XLA Ops:
  7.2 0.0 reduce-scatter.2.cloned.1.call-start
  7.2 4.8 copy_convert_fusion
  12.0 36.0 %slice.132 = f32[16,8,2048]{2,0,1:T(8,128)S(1)} slice(f32[16,16,4096]{2,0,1:T(8,128)} %copy_convert_fusion), slice={[0:16:1], [0:16:2], [0:4096:2]} | slice | bytes 2097152 | tf_op jit(solution)/shard_map/slice | solution.py:27
  48.0 36.0 %slice.133 = f32[16,8,2048]{2,0,1:T(8,128)S(1)} slice(f32[16,16,4096]{2,0,1:T(8,128)} %copy_convert_fusion), slice={[0:16:1], [0:16:2], [1:4096:2]} | slice | bytes 2097152 | tf_op jit(solution)/shard_map/slice | solution.py:28
  84.0 36.6 %slice.134 = f32[16,8,2048]{2,0,1:T(8,128)} slice(f32[16,16,4096]{2,0,1:T(8,128)} %copy_convert_fusion), slice={[0:16:1], [1:16:2], [0:4096:2]} | slice | bytes 2097152 | tf_op jit(solution)/shard_map/slice | solution.py:29
  120.5 47.9 %slice.135 = f32[16,8,2048]{2,0,1:T(8,128)} slice(f32[16,16,4096]{2,0,1:T(8,128)} %copy_convert_fusion), slice={[0:16:1], [1:16:2], [1:4096:2]} | slice | bytes 2097152 | tf_op jit(solution)/shard_map/slice | solution.py:30
  168.5 2.0 multiply_bitcast_fusion.2
  170.4 0.0 copy-start.1
  170.4 0.0 copy-start.2
  170.4 0.3 pad_maximum_fusion
  170.8 0.0 copy-start
  170.8 0.0 copy-start.5
  170.8 1.9 fusion.23
  172.7 5.0 collective-permute-start
  177.7 1.9 collective-permute-start.1
  179.7 0.0 copy-done
  179.7 0.0 copy-done.5
  179.7 5.8 fusion.2
  185.5 8.5 %copy.55 = f32[64,8,8,512]{3,2,1,0:T(8,128)S(1)} copy(f32[64,8,8,512]{3,1,2,0:T(8,128)S(1)} %bitcast.70) | data formatting | bytes 16777216
  194.0 8.1 %copy.51 = f32[1,32,16,8,512]{4,2,1,0,3:T(8,128)} copy(f32[1,32,16,8,512]{4,3,1,2,0:T(8,128)S(1)} %bitcast.67) | data formatting | bytes 16777216 | tf_op jit(solution)/shard_map/stack | solution.py:108
  202.1 0.0 collective-permute-done
  202.1 0.0 collective-permute-done.1
  202.1 0.0 copy-done.1
  202.1 6.9 fusion
  209.0 37.9 %slice_add_fusion = (f32[3,16,16,2048]{3,1,2,0:T(8,128)}, f32[3,16,16,2048]{3,1,2,0:T(8,128)}, f32[3,16,16,2048]{3,1,2,0:T(8,128)}, f32[3,16,16,2048]{3,1,2,0:T(8,128)}) fusion(f32[3,16,16,2056]{3,1,2,0:T(8,128)} %fusion), kind=kLoop, calls=%fused_computation.10 | loop fusion | flops 12582912 | bytes 81788928 | tf_op jit(solution)/shard_map/add | solution.py:55
  246.9 27.4 %fusion.8 = f32[3,16,8,2048]{3,1,2,0:T(8,128)S(1)} fusion(f32[3,16,16,2048]{3,1,2,0:T(8,128)} %get-tuple-element.4, f32[3,16,16,2048]{3,1,2,0:T(8,128)} %get-tuple-element.5, f32[3,16,16,2048]{3,1,2,0:T(8,128)} %get-tuple-element.6, f32[3,16,16,2048]{3,1,2,0:T(8,128)} %get-tuple-element.7, f32[1,16,8,2048]{3,1,2,0:T(8,128)} %copy-done.1, ...), kind=kLoop, calls=%fused_computation.26 | loop fusion | flops 25165824 | bytes 81788928 | tf_op jit(solution)/shard_map/mul | solution.py:102
  274.3 0.5 multiply_convert_fusion.3
  274.9 1.2 pad_maximum_fusion.1
  276.0 9.6 %copy.45 = bf16[16,8,2048,2]{0,1,3,2:T(8,128)(2,1)} copy(bf16[16,8,2048,2]{2,0,1,3:T(8,128)(2,1)} %get-tuple-element.19) | data formatting | bytes 2097152 | tf_op jit(solution)/shard_map/stack | solution.py:43
  285.6 9.4 %copy.47 = bf16[16,8,1,4096]{3,1,2,0:T(8,128)(2,1)} copy(bf16[16,8,1,4096]{0,1,3,2:T(8,128)(2,1)} %bitcast.65) | data formatting | bytes 2097152 | tf_op jit(solution)/shard_map/stack;reshape | solution.py:45
  295.0 8.5 %copy.46 = bf16[16,8,2048,2]{0,1,3,2:T(8,128)(2,1)} copy(bf16[16,8,2048,2]{2,0,1,3:T(8,128)(2,1)S(1)} %get-tuple-element.20) | data formatting | bytes 2097152 | tf_op jit(solution)/shard_map/stack | solution.py:44
  303.5 9.9 %copy.48 = bf16[16,8,1,4096]{3,1,2,0:T(8,128)(2,1)} copy(bf16[16,8,1,4096]{0,1,3,2:T(8,128)(2,1)} %bitcast.66) | data formatting | bytes 2097152 | tf_op jit(solution)/shard_map/stack;reshape | solution.py:45
  313.4 1.5 maximum_convert_fusion
  314.9 2.4 copy.49
  317.3 1.5 bitcast_multiply_fusion
  318.8 3.7 fusion.17
  322.5 8.3 %copy.54 = f32[64,8,8,512]{3,2,1,0:T(8,128)S(1)} copy(f32[64,8,8,512]{3,1,2,0:T(8,128)S(1)} %bitcast.68) | data formatting | bytes 16777216
  330.8 4.9 copy.50
  335.7 10.3 %maximum_bitcast_fusion = f32[8,2,32,16,512]{4,3,2,1,0:T(8,128)} fusion(f32[1,32,16,8,512]{4,2,1,0,3:T(8,128)} %copy.51, f32[1,32,16,8,512]{4,2,1,0,3:T(8,128)S(1)} %copy.50), kind=kLoop, calls=%fused_computation.1 | loop fusion | flops 4194304 | bytes 33554432 | tf_op jit(solution)/shard_map/transpose | solution.py:111
  346.0 0.0 reduce-scatter.2.cloned.1.call-update
  346.1 328.6 %reduce-scatter.2.cloned.1.call-done = f32[1,2,32,16,512]{4,3,2,1,0:T(8,128)} async-done(((f32[8,2,32,16,512]{4,3,2,1,0:T(8,128)}), f32[1,2,32,16,512]{4,3,2,1,0:T(8,128)}) %reduce-scatter.2.cloned.1.call-update) | async-done | bytes 2097168 | tf_op jit(solution)/shard_map/reduce_scatter | solution.py:110
  674.6 1.9 fusion.21
  676.5 1.5 convolution_bitcast_fusion
  678.0 66.0 %all-reduce.1 = (f32[32,32]{1,0:T(8,128)S(1)}, f32[32]{0:T(128)S(1)}) all-reduce(f32[32,32]{1,0:T(8,128)S(1)} %convolution_bitcast_fusion, f32[32]{0:T(128)S(1)} %get-tuple-element.17), channel_id=1, replica_groups=mesh['photo'=8,'tile'=16] {'photo','tile'}, use_global_device_ids=true, to_apply=%region_1.2 | all-reduce | flops 1056 | bytes 8448 | tf_op jit(solution)/shard_map/psum | solution.py:121
  744.1 0.1 multiply_subtract_fusion
  744.1 0.7 gather_fusion
  744.9 0.7 rsqrt_multiply_fusion
  745.5 0.0 copy-done.3
  (7 shorter events, 0.0 us)
Async XLA Ops:
  7.2 667.5 %reduce-scatter.2.cloned.1.call-start = ((), (), s32[]{:S(2)}) async-start(), calls=%async_computation.1 | async-start | bytes 18874368 | tf_op jit(solution)/shard_map/reduce_scatter | solution.py:110
  170.4 31.6 %copy-start.1 = (f32[1,16,8,2048]{3,1,2,0:T(8,128)}, f32[1,16,8,2048]{3,1,2,0:T(8,128)S(1)}, u32[]{:S(2)}) copy-start(f32[1,16,8,2048]{3,1,2,0:T(8,128)S(1)} %get-tuple-element.9) | copy-start | bytes 3145732
  170.4 31.6 %copy-start.2 = (f32[1,16,8,2048]{3,1,2,0:T(8,128)}, f32[1,16,8,2048]{3,1,2,0:T(8,128)S(1)}, u32[]{:S(2)}) copy-start(f32[1,16,8,2048]{3,1,2,0:T(8,128)S(1)} %get-tuple-element.10) | copy-start | bytes 3145732
  170.8 8.9 %copy-start = (bf16[16,16,4096]{2,1,0:T(8,128)(2,1)S(1)}, bf16[16,16,4096]{2,1,0:T(8,128)(2,1)}, u32[]{:S(2)}) copy-start(bf16[16,16,4096]{2,1,0:T(8,128)(2,1)} %param.2) | copy-start | bytes 6291460
  170.8 8.9 %copy-start.5 = (s32[16]{0:T(128)S(1)}, s32[16]{0:T(128)}, u32[]{:S(2)}) copy-start(s32[16]{0:T(128)} %param.3) | copy-start | bytes 196
  172.7 29.4 %collective-permute-start = (f32[3,16,4,2048]{3,1,2,0:T(8,128)}, f32[3,16,4,2048]{3,1,2,0:T(8,128)}, u32[]{:S(2)}, u32[]{:S(2)}) collective-permute-start(f32[3,16,4,2048]{3,1,2,0:T(8,128)} %get-tuple-element.15), channel_id=1, source_target_pairs={{0,1},{1,2},{2,3},{3,4},{4,5},{5,6},{6,7},{7,8},{8,9},{9,10},{10,1... | collective-permute-start | bytes 4718600 | tf_op jit(solution)/shard_map/ppermute | solution.py:20
  177.7 24.3 %collective-permute-start.1 = (f32[3,16,4,2048]{3,1,2,0:T(8,128)}, f32[3,16,4,2048]{3,1,2,0:T(8,128)}, u32[]{:S(2)}, u32[]{:S(2)}) collective-permute-start(f32[3,16,4,2048]{3,1,2,0:T(8,128)} %get-tuple-element.16), channel_id=1, source_target_pairs={{1,0},{2,1},{3,2},{4,3},{5,4},{6,5},{7,6},{8,7},{9,8},{10,9},{11,1... | collective-permute-start | bytes 4718600 | tf_op jit(solution)/shard_map/ppermute | solution.py:21
  303.5 9.9 %copy-start.4 = (bf16[16,8,1,4096]{3,1,2,0:T(8,128)(2,1)S(1)}, bf16[16,8,1,4096]{3,1,2,0:T(8,128)(2,1)}, u32[]{:S(2)}) copy-start(bf16[16,8,1,4096]{3,1,2,0:T(8,128)(2,1)} %copy.47) | copy-start | bytes 3145732
  676.5 69.0 %copy-start.3 = (f32[32,16,512]{2,1,0:T(8,128)}, f32[32,16,512]{2,1,0:T(8,128)S(1)}, u32[]{:S(2)}) copy-start(f32[32,16,512]{2,1,0:T(8,128)S(1)} %get-tuple-element.18) | copy-start | bytes 3145732
Sparse Core Ops, SparseCore 0:
  346.2 328.4 reduce-scatter.1
where the time goes:
time: 762 us; the launch traced here: 753 us
  waiting for transfers between devices  329 us (43%)
  local copies, waits for them, and re-layouts  229 us (30%)
  other arithmetic  96.9 us (13%)
  blocking collectives  66 us (9%)
  between operations  14.4 us (2%)
  matrix products  11 us (1%)
    reduce_scatter x1, waiting for transfers between devices, on_device(): lax.psum_scatter(jnp.transpose(stacked, (3, 0, 1, 2, 4)), 'photo', scatte...  329 us
    psum x1, blocking collectives, on_device(): gram, totals = lax.psum((gram_local, totals_local), ('photo', 'tile'))  66 us
    slice x1, local copies, waits for them, and re-layouts, forward_haar(): low_right = field[..., 1::2, 1::2]  47.9 us
    add x1, other arithmetic, local_variance(): column_box + squares[..., :, 4 - radius:4 - radius + cols]  37.9 us
    slice x1, local copies, waits for them, and re-layouts, forward_haar(): low_left = field[..., 1::2, 0::2]  36.6 us
    slice x1, local copies, waits for them, and re-layouts, forward_haar(): top_left = field[..., 0::2, 0::2]  36 us
    slice x1, local copies, waits for them, and re-layouts, forward_haar(): top_right = field[..., 0::2, 1::2]  36 us
    mul x1, other arithmetic, on_device(): noise_map = inverse_haar(centre * gain).astype(jnp.bfloat16)  27.4 us
  transfers between devices with their start and end apart: 3, of which 1 were waited for; matrix products, arithmetic and copies ran while one was open for 3% of the time, Pallas kernels for 0%

commit v1 on v0

v1 whole, which is shorter than its diff:
```python
import functools

import jax
import jax.numpy as jnp
import numpy as np
from jax import lax
from jax.experimental import pallas as pl
from jax.experimental.pallas import tpu as pltpu
from jax.sharding import PartitionSpec as P

MESH = pl.DeviceIdType.MESH
F32 = jnp.float32
BF16 = jnp.bfloat16

CAMS = 32
NOISE_POWER = 1.0
VAR_EPS = 1e-06

PH = 8
TI = 16
OWN = 16
HR = 8
LANES = 1152
VMEM_LIMIT = 60 * 1024 * 1024


def constants():
    perm = np.zeros((256, 256), np.float32)
    for tb in range(2):
        for i in range(HR):
            for p in range(OWN):
                perm[(tb * HR + i) * OWN + p, p * 16 + 2 * i + tb] = 1.0
    edge = np.zeros((2, 2, 256, 128), np.float32)
    for tb in range(2):
        for k in range(8):
            edge[tb, 0, 248 + k, 16 * tb + k] = 1.0
            edge[tb, 1, k, 16 * tb + 8 + k] = 1.0
    sign = np.array([[1, 1, 1], [1, -1, -1], [-1, 1, -1], [-1, -1, 1]], np.float32) * 0.5
    haar = np.zeros((512, 384), np.float32)
    for j in range(128):
        for b in range(3):
            haar[2 * j, 128 * b + j] = sign[0, b]
            haar[2 * j + 1, 128 * b + j] = sign[1, b]
            haar[256 + 2 * j, 128 * b + j] = sign[2, b]
            haar[256 + 2 * j + 1, 128 * b + j] = sign[3, b]
    haar_edge = np.zeros((128, 128), np.float32)
    for k in range(8):
        for b in range(3):
            haar_edge[2 * k, 8 * b + k] = sign[0, b]
            haar_edge[2 * k + 1, 8 * b + k] = sign[1, b]
            haar_edge[16 + 2 * k, 8 * b + k] = sign[2, b]
            haar_edge[16 + 2 * k + 1, 8 * b + k] = sign[3, b]
    split = np.zeros((256, 256), np.float32)
    for j in range(128):
        split[2 * j, j] = 1.0
        split[2 * j + 1, 128 + j] = 1.0
    out = np.arange(256)
    box = np.zeros((4, 3, 768, 256), np.float32)
    for r in range(1, 5):
        inner = (np.abs(out[:, None] - out[None, :]) <= r).astype(np.float32)
        for b in range(3):
            side = np.zeros((128, 256), np.float32)
            for k in range(8):
                cell = k - 4 if k < 4 else 252 + k
                side[8 * b + k] = np.abs(cell - out) <= r
            box[r - 1, b] = np.concatenate([inner, inner, side, side])
    return [jnp.asarray(c, BF16) for c in (perm, edge, haar, haar_edge, split, box)]


def dot(a, b):
    return jnp.dot(a, b, preferred_element_type=F32)


def hi_lo(x):
    hi = x.astype(BF16)
    lo = (x - hi.astype(F32)).astype(BF16)
    return hi, lo


def pack_kernel(x_ref, perm_ref, edge_ref, out_ref, y_ref):
    perm = perm_ref[...]
    for c in range(16):
        x = x_ref[:, :, 256 * c : 256 * c + 256].reshape(256, 256)
        y = dot(perm, x).astype(BF16)
        y_ref[c] = y
        d, ct = divmod(c, 2)
        for tb in range(2):
            lane = ct * 512 + tb * 256
            out_ref[d, :, :, lane : lane + 256] = y[tb * 128 : tb * 128 + 128].reshape(HR, OWN, 256)
    for d in range(PH):
        side = jnp.zeros((128, 128), F32)
        for tb in range(2):
            if d > 0:
                side += dot(y_ref[2 * d - 1, pl.ds(tb * 128, 128), :], edge_ref[tb, 0])
            if d < PH - 1:
                side += dot(y_ref[2 * d + 2, pl.ds(tb * 128, 128), :], edge_ref[tb, 1])
        out_ref[d, :, :, 1024:1152] = side.astype(BF16).reshape(HR, OWN, 128)


def packed(photos, perm, edge):
    return pl.pallas_call(
        pack_kernel,
        out_shape=jax.ShapeDtypeStruct((PH, HR, OWN, LANES), BF16),
        in_specs=[pl.BlockSpec(memory_space=pltpu.VMEM)] * 3,
        out_specs=pl.BlockSpec(memory_space=pltpu.VMEM),
        scratch_shapes=[pltpu.VMEM((16, 256, 256), BF16)],
        compiler_params=pltpu.CompilerParams(vmem_limit_bytes=VMEM_LIMIT),
        name="pack",
    )(photos, perm, edge)


def exchange_kernel(
    ext_ref, idr_ref, main_ref, top_ref, bot_ref, ids_ref,
    own_sem, send_sem, recv_sem, isend_sem, irecv_sem, up_send, up_recv, dn_send, dn_recv,
):
    me = lax.axis_index("photo")
    t = lax.axis_index("tile")

    barrier = pltpu.get_barrier_semaphore()
    for k in range(1, PH):
        peer = lax.rem(me + k, PH)
        pl.semaphore_signal(barrier, inc=1, device_id={"photo": peer}, device_id_type=MESH)

    for k in (1, TI - 1):
        pl.semaphore_signal(
            barrier, inc=1, device_id={"tile": lax.rem(t + k, TI)}, device_id_type=MESH
        )
    pl.semaphore_wait(barrier, PH + 1)

    def a2a(k):
        peer = lax.rem(me + k, PH)
        return pltpu.make_async_remote_copy(
            src_ref=ext_ref.at[peer], dst_ref=main_ref.at[me],
            send_sem=send_sem.at[k - 1], recv_sem=recv_sem.at[k - 1],
            device_id={"photo": peer}, device_id_type=MESH,
        )

    def idc(k):
        peer = lax.rem(me + k, PH)
        return pltpu.make_async_remote_copy(
            src_ref=idr_ref, dst_ref=ids_ref.at[me],
            send_sem=isend_sem.at[k - 1], recv_sem=irecv_sem.at[k - 1],
            device_id={"photo": peer}, device_id_type=MESH,
        )

    def up(k, src, s):
        return pltpu.make_async_remote_copy(
            src_ref=src.at[s, pl.ds(0, 4)], dst_ref=bot_ref.at[s],
            send_sem=up_send.at[k], recv_sem=up_recv.at[k],
            device_id={"tile": t - 1}, device_id_type=MESH,
        )

    def down(k, src, s):
        return pltpu.make_async_remote_copy(
            src_ref=src.at[s, pl.ds(4, 4)], dst_ref=top_ref.at[s],
            send_sem=dn_send.at[k], recv_sem=dn_recv.at[k],
            device_id={"tile": t + 1}, device_id_type=MESH,
        )

    def pass_on(k, src, s):
        @pl.when(t > 0)
        def _():
            up(k, src, s).start()

        @pl.when(t < TI - 1)
        def _():
            down(k, src, s).start()

    for k in range(1, PH):
        a2a(k).start()
    for k in range(1, PH):
        idc(k).start()
    pass_on(0, ext_ref, me)
    own = pltpu.make_async_copy(ext_ref.at[me], main_ref.at[me], own_sem.at[0])
    own.start()
    own_id = pltpu.make_async_copy(idr_ref, ids_ref.at[me], own_sem.at[1])
    own_id.start()

    @pl.when(t == 0)
    def _():
        top_ref[...] = jnp.zeros(top_ref.shape, BF16)

    @pl.when(t == TI - 1)
    def _():
        bot_ref[...] = jnp.zeros(bot_ref.shape, BF16)

    for k in range(1, PH):
        s = lax.rem(me + PH - k, PH)
        a2a(k).wait_recv()
        pass_on(k, main_ref, s)
    for k in range(1, PH):
        a2a(k).wait_send()
        idc(k).wait()
    own.wait()
    own_id.wait()

    @pl.when(t > 0)
    def _():
        for k in range(PH):
            s = lax.rem(me + PH - k, PH)
            up(k, main_ref, s).wait_send()
            down(k, main_ref, s).wait_recv()

    @pl.when(t < TI - 1)
    def _():
        for k in range(PH):
            s = lax.rem(me + PH - k, PH)
            down(k, main_ref, s).wait_send()
            up(k, main_ref, s).wait_recv()


def exchanged(ext, idr):
    vm = pl.BlockSpec(memory_space=pltpu.VMEM)
    dma = pltpu.SemaphoreType.DMA
    return pl.pallas_call(
        exchange_kernel,
        out_shape=(
            jax.ShapeDtypeStruct((PH, HR, OWN, LANES), BF16),
            jax.ShapeDtypeStruct((PH, 4, OWN, LANES), BF16),
            jax.ShapeDtypeStruct((PH, 4, OWN, LANES), BF16),
            jax.ShapeDtypeStruct((PH, 8, 128), jnp.int32),
        ),
        in_specs=[vm] * 2,
        out_specs=(vm,) * 4,
        scratch_shapes=[
            dma((2,)), dma((PH - 1,)), dma((PH - 1,)), dma((PH - 1,)), dma((PH - 1,)),
            dma((PH,)), dma((PH,)), dma((PH,)), dma((PH,)),
        ],
        compiler_params=pltpu.CompilerParams(
            collective_id=0, has_side_effects=True, vmem_limit_bytes=VMEM_LIMIT
        ),
        name="exchange",
    )(ext, idr)


def bands_of(x, rows, sq_ref, eq_ref, band_ref, s2, first, haar, haar_edge):
    m = rows * OWN
    for ct in range(2):
        got = dot(x[:, :, 512 * ct : 512 * ct + 512].reshape(m, 512), haar)
        for b in range(3):
            one = got[:, 128 * b : 128 * b + 128].reshape(rows, OWN, 128)
            if band_ref is not None:
                band_ref[b, s2, :, :, 128 * ct : 128 * ct + 128] = one
            sq_ref[b, s2, first : first + rows, :, 128 * ct : 128 * ct + 128] = one * one
    edge = dot(x[:, :, 1024:1152].reshape(m, 128), haar_edge).reshape(rows, OWN, 128)
    eq_ref[s2, first : first + rows] = edge * edge


def chunk(k, main_ref, top_ref, bot_ref, ids_ref, consts, scratch):
    haar_ref, haar_edge_ref, split_ref, box_ref = consts
    sq_ref, eq_ref, band_ref, lhs_ref, sum_ref, px_ref, data_ref, acc_ref = scratch
    haar, haar_edge = haar_ref[...], haar_edge_ref[...]
    for s2 in range(2):
        s = 2 * k + s2
        bands_of(top_ref[s], 4, sq_ref, eq_ref, None, s2, 0, haar, haar_edge)
        bands_of(main_ref[s], HR, sq_ref, eq_ref, band_ref, s2, 4, haar, haar_edge)
        bands_of(bot_ref[s], 4, sq_ref, eq_ref, None, s2, 12, haar, haar_edge)
        for ct in range(2):
            for tb in range(2):
                lane = 512 * ct + 256 * tb
                x = main_ref[s, :, :, lane : lane + 256].reshape(HR * OWN, 256)
                got = dot(x, split_ref[...])
                for odd in range(2):
                    px_ref[2 * tb + odd, s2, :, :, 128 * ct : 128 * ct + 128] = got[
                        :, 128 * odd : 128 * odd + 128
                    ].reshape(HR, OWN, 128)

    def sums(n, _):
        s2, i = n // HR, lax.rem(n, HR)
        row = eq_ref[s2, i + 4]
        for r in range(1, 5):
            row = row + eq_ref[s2, i + 4 - r] + eq_ref[s2, i + 4 + r]
            hi, lo = hi_lo(row)
            for b in range(3):
                lhs_ref[r - 1, b, n, :, 512:640] = hi
                lhs_ref[r - 1, b, n, :, 640:768] = lo
        for b in range(3):
            row = sq_ref[b, s2, i + 4]
            for r in range(1, 5):
                row = row + sq_ref[b, s2, i + 4 - r] + sq_ref[b, s2, i + 4 + r]
                hi, lo = hi_lo(row)
                lhs_ref[r - 1, b, n, :, 0:256] = hi
                lhs_ref[r - 1, b, n, :, 256:512] = lo
        return 0

    lax.fori_loop(0, 2 * HR, sums, 0)

    for r in range(4):
        for b in range(3):
            got = dot(lhs_ref[r, b].reshape(256, 768), box_ref[r, b])
            sum_ref[r, b] = got.reshape(2 * HR, OWN, 256)

    def residual(n, _):
        s2, i = n // HR, lax.rem(n, HR)
        res = []
        for b in range(3):
            var = sum_ref[0, b, n] * (1.0 / 9.0)
            for r in range(1, 4):
                var = jnp.minimum(var, sum_ref[r, b, n] * (1.0 / (2 * r + 3) ** 2))
            gain = NOISE_POWER / jnp.maximum(var, NOISE_POWER)
            res.append(band_ref[b, s2, i] * gain * 0.5)
        hz, vt, dg = res
        plus, minus = hz + vt, hz - vt
        noise = (plus + dg, minus - dg, -minus - dg, dg - plus)
        at = pl.multiple_of(n * OWN, OWN)
        for j in range(4):
            x = px_ref[j, s2, i]
            for part, value in enumerate((noise[j].astype(BF16).astype(F32) * x, x * x)):
                hi, lo = hi_lo(value)
                data_ref[2 * j + part, pl.ds(at, OWN), :] = hi
                data_ref[2 * j + part, pl.ds(256 + at, OWN), :] = lo
        return 0

    lax.fori_loop(0, 2 * HR, residual, 0)

    ids = jnp.concatenate([ids_ref[2 * k, 0:1, :], ids_ref[2 * k + 1, 0:1, :]], axis=1)
    row = lax.broadcasted_iota(jnp.int32, (256, 256), 0)
    col = lax.broadcasted_iota(jnp.int32, (256, 256), 1)
    same = (row // HR == ids) & (lax.rem(row, HR) == lax.rem(col // OWN, HR))
    pick = jnp.where(same, 1.0, 0.0).astype(BF16)
    pick = jnp.concatenate([pick, pick], axis=1)
    for j in range(8):
        acc_ref[j] += dot(pick, data_ref[j])


def three(x):
    hi = x.astype(BF16)
    rest = x - hi.astype(F32)
    mid = rest.astype(BF16)
    low = (rest - mid.astype(F32)).astype(BF16)
    return jnp.concatenate([hi, mid, low], axis=1)


def finish(acc_ref, join_ref, rows_ref, fp_ref):
    for tb in range(2):
        for ct in range(2):
            pair = []
            for odd in range(2):
                j = 2 * tb + odd
                lanes = pl.ds(128 * ct, 128)
                pair.append(acc_ref[2 * j, :, lanes] / acc_ref[2 * j + 1, :, lanes])
            got = dot(three(jnp.concatenate(pair, axis=1)), join_ref[...])
            for part in range(2):
                one = got[:, 128 * part : 128 * part + 128].reshape(CAMS, HR, 128)
                rows_ref[2 * ct + part, :, pl.ds(tb, HR, stride=2), :] = one
    for part in range(4):
        fp_ref[:, :, 128 * part : 128 * part + 128] = rows_ref[part]


def compute_kernel(
    main_ref, top_ref, bot_ref, ids_ref, haar_ref, haar_edge_ref, split_ref, join_ref, box_ref,
    fp_ref, *scratch,
):
    *scratch, rows_ref = scratch
    acc_ref = scratch[-1]
    acc_ref[...] = jnp.zeros(acc_ref.shape, F32)
    consts = (haar_ref, haar_edge_ref, split_ref, box_ref)

    def step(k, _):
        chunk(k, main_ref, top_ref, bot_ref, ids_ref, consts, scratch)
        return 0

    lax.fori_loop(0, PH // 2, step, 0)
    finish(acc_ref, join_ref, rows_ref, fp_ref)


SCRATCH = [
    ((3, 2, 16, OWN, 256), F32),
    ((2, 16, OWN, 128), F32),
    ((3, 2, HR, OWN, 256), F32),
    ((4, 3, 2 * HR, OWN, 768), BF16),
    ((4, 3, 2 * HR, OWN, 256), F32),
    ((4, 2, HR, OWN, 256), F32),
    ((8, 512, 256), BF16),
    ((8, 256, 256), F32),
    ((4, CAMS, 16, 128), F32),
]


def computed(main, top, bot, ids, haar, haar_edge, split, join, box):
    vm = pl.BlockSpec(memory_space=pltpu.VMEM)
    return pl.pallas_call(
        compute_kernel,
        out_shape=jax.ShapeDtypeStruct((CAMS, 16, 512), F32),
        in_specs=[vm] * 9,
        out_specs=vm,
        scratch_shapes=[pltpu.VMEM(s, d) for s, d in SCRATCH],
        compiler_params=pltpu.CompilerParams(vmem_limit_bytes=VMEM_LIMIT),
        name="residuals",
    )(main, top, bot, ids, haar, haar_edge, split, join, box)


def allsum_kernel(x_ref, o_ref, a_ref, m_ref, b_ref, own_sem, as_sem, ar_sem, bs_sem, br_sem):
    me = lax.axis_index("photo")
    t = lax.axis_index("tile")
    barrier = pltpu.get_barrier_semaphore()
    for k in range(1, PH):
        pl.semaphore_signal(
            barrier, inc=1, device_id={"photo": lax.rem(me + k, PH)}, device_id_type=MESH
        )
    for k in range(1, TI):
        pl.semaphore_signal(
            barrier, inc=1, device_id={"tile": lax.rem(t + k, TI)}, device_id_type=MESH
        )
    pl.semaphore_wait(barrier, PH + TI - 2)

    def first(k):
        return pltpu.make_async_remote_copy(
            src_ref=x_ref, dst_ref=a_ref.at[k - 1], send_sem=as_sem.at[k - 1],
            recv_sem=ar_sem.at[k - 1],
            device_id={"photo": lax.rem(me + k, PH)}, device_id_type=MESH,
        )

    def second(k):
        return pltpu.make_async_remote_copy(
            src_ref=m_ref, dst_ref=b_ref.at[k - 1], send_sem=bs_sem.at[k - 1],
            recv_sem=br_sem.at[k - 1],
            device_id={"tile": lax.rem(t + k, TI)}, device_id_type=MESH,
        )

    for k in range(1, PH):
        first(k).start()
    for k in range(1, PH):
        first(k).wait_recv()
    total = jnp.zeros(x_ref.shape, F32)
    for s in range(PH):
        k = lax.rem(me + PH - s, PH)
        other = a_ref[jnp.maximum(k - 1, 0)]
        total += jnp.where(k == 0, x_ref[...], other)
    m_ref[...] = total
    for k in range(1, TI):
        second(k).start()
    for k in range(1, TI):
        second(k).wait_recv()
    total = jnp.zeros(x_ref.shape, F32)
    for s in range(TI):
        k = lax.rem(t + TI - s, TI)
        other = b_ref[jnp.maximum(k - 1, 0)]
        total += jnp.where(k == 0, m_ref[...], other)
    o_ref[...] = total
    for k in range(1, PH):
        first(k).wait_send()
    for k in range(1, TI):
        second(k).wait_send()


def allsum(x):
    vm = pl.BlockSpec(memory_space=pltpu.VMEM)
    dma = pltpu.SemaphoreType.DMA
    return pl.pallas_call(
        allsum_kernel,
        out_shape=jax.ShapeDtypeStruct(x.shape, F32),
        in_specs=[vm],
        out_specs=vm,
        scratch_shapes=[
            pltpu.VMEM((PH - 1,) + x.shape, F32),
            pltpu.VMEM(x.shape, F32),
            pltpu.VMEM((TI - 1,) + x.shape, F32),
            dma((1,)), dma((PH - 1,)), dma((PH - 1,)), dma((TI - 1,)), dma((TI - 1,)),
        ],
        compiler_params=pltpu.CompilerParams(collective_id=1, has_side_effects=True),
        name="allsum",
    )(x)


def on_device(photos, camera_id):
    perm, edge, haar, haar_edge, split, box = constants()
    join = jnp.concatenate([split.T] * 3)
    ext = packed(photos, perm, edge)
    idr = jnp.broadcast_to(jnp.tile(camera_id, HR)[None, :], (8, 128))
    main, top, bot, ids = exchanged(ext, idr)
    fingerprints = computed(main, top, bot, ids, haar, haar_edge, split, join, box)
    flat = fingerprints.reshape(CAMS, -1)
    gram_local = jnp.dot(flat, flat.T, precision=lax.Precision.HIGHEST, preferred_element_type=F32)
    totals_local = jnp.sum(flat, axis=1)
    both = jnp.zeros((CAMS, 128), F32)
    both = both.at[:, :CAMS].set(gram_local).at[:, CAMS].set(totals_local)
    both = allsum(both)
    pixels = float(256 * 4096)
    average = both[:, CAMS] / pixels
    covar = both[:, :CAMS] / pixels - average[:, None] * average[None, :]
    spread = jnp.diagonal(covar) + VAR_EPS
    correlation = covar / jnp.sqrt(spread[:, None] * spread[None, :])
    return (fingerprints, correlation)


def solution(mesh):
    return jax.shard_map(
        on_device,
        mesh=mesh,
        in_specs=(P("photo", "tile", None), P("photo")),
        out_specs=(P(None, "tile", "photo"), P()),
        check_vma=False,
    )
```

time: 762 us -> 112 us (0.15); the launches traced: 753 us -> 111 us
  waiting for transfers between devices: 329 us -> 0 us
  local copies, waits for them, and re-layouts: 229 us -> 2.22 us
  Pallas kernels: 0 us -> 97.4 us
  other arithmetic: 96.9 us -> 6.59 us
  blocking collectives: 66 us -> 0 us
  between operations: 14.4 us -> 0.7 us
    reduce_scatter x1 -> x0, waiting for transfers between devices: 329 us -> none  [on_device(): lax.psum_scatter(jnp.transpose(stacked, (3, 0, 1, 2, 4)), 'photo', scatte...]
    slice x5 -> x0, local copies, waits for them, and re-layouts: 158 us -> none  [the longest x1 47.9 us: forward_haar(): low_right = field[..., 1::2, 1::2]]
    pallas_call x0 -> x4, Pallas kernels: none -> 97.4 us  [the longest x1 46.4 us: exchanged(): pl.pallas_call(exchange_kernel, out_shape=(jax.ShapeDtypeStruct((PH, HR,...]
    psum x1 -> x0, blocking collectives: 66 us -> none  [on_device(): gram, totals = lax.psum((gram_local, totals_local), ('photo', 'tile'))]
    another operation x6 -> x2, local copies, waits for them, and re-layouts: 50.3 us -> 0.09 us  [the longest x2 19.3 us: inverse_haar(): joined = jnp.stack([upper, lower], -2)]
    add x2 -> x1, other arithmetic: 37.9 us -> 0.01 us  [on_device(): spread = jnp.diagonal(covar) + VAR_EPS]
    mul x3 -> x0, other arithmetic: 35.8 us -> none  [the longest x1 27.4 us: on_device(): noise_map = inverse_haar(centre * gain).astype(jnp.bfloat16)]
    unnamed x14 -> x4, local copies, waits for them, and re-layouts: 16.8 us -> 0.6 us
  transfers between devices with their start and end apart: 3 -> 0, of which waited for: 1 -> 0; matrix products, arithmetic and copies ran while one was open for 3% -> 0% of each run, Pallas kernels for 0% -> 0%
where the time goes in v1:
time: 112 us; the launch traced here: 111 us
  Pallas kernels  97.4 us (87%)
  other arithmetic  6.59 us (6%)
  matrix products  4.33 us (4%)
  local copies, waits for them, and re-layouts  2.22 us (2%)
    pallas_call x1, Pallas kernels, exchanged(): pl.pallas_call(exchange_kernel, out_shape=(jax.ShapeDtypeStruct((PH, HR,...  46.4 us
    pallas_call x1, Pallas kernels, computed(): pl.pallas_call(compute_kernel, out_shape=jax.ShapeDtypeStruct((CAMS, 16,...  25.9 us
    pallas_call x1, Pallas kernels, allsum(): pl.pallas_call(allsum_kernel, out_shape=jax.ShapeDtypeStruct(x.shape, F32...  20.8 us
    dot_general x1, matrix products, on_device(): jnp.dot(flat, flat.T, precision=lax.Precision.HIGHEST, preferred_element_...  4.33 us
    pallas_call x1, Pallas kernels, packed(): pl.pallas_call(pack_kernel, out_shape=jax.ShapeDtypeStruct((PH, HR, OWN,...  4.29 us

profile of v1, /device:TPU:1, one launch (start us, length us, event | category | flops | bytes accessed | tf_op | source)
XLA Modules:
  0.0 111.3 jit_solution(6769975462405790345)
XLA Ops:
  0.6 0.0 copy-start.1
  0.6 4.3 %pack.1.ext_ref = bf16[8,8,16,1152]{3,2,1,0:T(8,128)(2,1)} custom-call(bf16[16,16,4096]{2,1,0:T(8,128)(2,1)} %x_ref.1, bf16[256,256]{1,0:T(8,128)(2,1)} %constant.84.clone.perm_ref, bf16[2,2,256,128]{3,2,1,0:T(8,128)(2,1)} %constant.85.clone.edge_ref), custom_call_target="tpu_custom_call" | custom-call | tf_op jit(solution)/shard_map/pack/pallas_call | solution.py:101
  4.9 0.0 copy-done.1
  4.9 0.1 broadcast_in_dim.6
  5.0 0.6 broadcast_in_dim.7.idr_ref
  5.6 46.4 %exchange.1 = (bf16[8,8,16,1152]{3,2,1,0:T(8,128)(2,1)}, bf16[8,4,16,1152]{3,2,1,0:T(8,128)(2,1)}, bf16[8,4,16,1152]{3,2,1,0:T(8,128)(2,1)}, s32[8,8,128]{2,1,0:T(8,128)}) custom-call(bf16[8,8,16,1152]{3,2,1,0:T(8,128)(2,1)} %pack.1.ext_ref, s32[8,128]{1,0:T(8,128)} %broadcast_in_dim.7.idr_ref), custom_call_target="tpu_custom_call" | custom-call | tf_op jit(solution)/shard_map/exchange/pallas_call | solution.py:215
  52.0 25.9 %residuals.1 = f32[32,16,512]{2,1,0:T(8,128)} custom-call(bf16[8,8,16,1152]{3,2,1,0:T(8,128)(2,1)} %get-tuple-element.30.main_ref, bf16[8,4,16,1152]{3,2,1,0:T(8,128)(2,1)} %get-tuple-element.31.top_ref, bf16[8,4,16,1152]{3,2,1,0:T(8,128)(2,1)} %get-tuple-element.32.bot_ref, s32[8,8,128]{2,1,0:T(8,128)} %get-tuple-element.33.ids_ref, ...), custom_call_target="tpu_custom_call" | custom-call | tf_op jit(solution)/shard_map/residuals/pallas_call | solution.py:382
  78.0 0.6 compare_reduce_fusion.1
  78.6 4.3 %fusion = f32[32,32]{1,0:T(8,128)S(1)} fusion(f32[32,16,512]{2,1,0:T(8,128)} %residuals.1, pred[]{:T(512)} %compare_reduce_fusion.1), kind=kOutput, calls=%fused_computation.2 | convolution fusion | flops 100664320 | bytes 1052673 | tf_op jit(solution)/shard_map/dot_general | solution.py:474
  82.9 1.6 %reduce_sum.9 = f32[32]{0:T(128)S(1)} reduce(f32[32,16,512]{2,1,0:T(8,128)} %residuals.1, f32[]{:T(128)} %constant.79.clone.1), dimensions={1,2}, to_apply=%region_2.0 | reduce | flops 262112 | bytes 1048708 | tf_op jit(solution)/shard_map/reduce_sum | solution.py:475
  84.5 0.6 compare_reduce_fusion
  85.1 0.6 fusion.2
  85.8 0.1 copy.15
  85.9 0.1 scatter.9.x_ref
  86.0 0.0 copy-start
  86.0 0.6 copy-done
  86.6 20.8 %allsum.1 = f32[32,128]{1,0:T(8,128)} custom-call(f32[32,128]{1,0:T(8,128)} %copy-done), custom_call_target="tpu_custom_call" | custom-call | tf_op jit(solution)/shard_map/allsum/pallas_call | solution.py:450
  107.4 0.9 multiply_reduce_fusion
  108.3 0.8 multiply_subtract_fusion
  109.1 0.7 gather_fusion
  109.9 1.4 %rsqrt_multiply_fusion = f32[32,32]{1,0:T(8,128)} fusion(f32[32]{0:T(128)S(1)} %broadcast_add_fusion, f32[32]{0:T(128)S(1)} %multiply_reduce_fusion, f32[32,128]{1,0:T(8,128)} %allsum.1), kind=kLoop, calls=%fused_computation.4 | loop fusion | flops 5120 | bytes 10240 | tf_op jit(solution)/shard_map/div | solution.py:483
  (4 shorter events, 0.0 us)
Async XLA Ops:
  0.6 4.3 %copy-start.1 = (s32[16]{0:T(128)S(1)}, s32[16]{0:T(128)}, u32[]{:S(2)}) copy-start(s32[16]{0:T(128)} %param.13) | copy-start | bytes 196
  86.0 0.6 copy-start

commit v2 on v1

v2 whole, which is shorter than its diff:
```python
import functools

import jax
import jax.numpy as jnp
import numpy as np
from jax import lax
from jax.experimental import pallas as pl
from jax.experimental.pallas import tpu as pltpu
from jax.sharding import PartitionSpec as P

MESH = pl.DeviceIdType.MESH
F32 = jnp.float32
BF16 = jnp.bfloat16

CAMS = 32
NOISE_POWER = 1.0
VAR_EPS = 1e-06

PH = 8
TI = 16
OWN = 16
HR = 8
LANES = 1152
VMEM_LIMIT = 60 * 1024 * 1024


def constants():
    perm = np.zeros((256, 256), np.float32)
    for tb in range(2):
        for i in range(HR):
            for p in range(OWN):
                perm[(tb * HR + i) * OWN + p, p * 16 + 2 * i + tb] = 1.0
    edge = np.zeros((2, 2, 256, 128), np.float32)
    for tb in range(2):
        for k in range(8):
            edge[tb, 0, 248 + k, 16 * tb + k] = 1.0
            edge[tb, 1, k, 16 * tb + 8 + k] = 1.0
    sign = np.array([[1, 1, 1], [1, -1, -1], [-1, 1, -1], [-1, -1, 1]], np.float32) * 0.5
    haar = np.zeros((512, 384), np.float32)
    for j in range(128):
        for b in range(3):
            haar[2 * j, 128 * b + j] = sign[0, b]
            haar[2 * j + 1, 128 * b + j] = sign[1, b]
            haar[256 + 2 * j, 128 * b + j] = sign[2, b]
            haar[256 + 2 * j + 1, 128 * b + j] = sign[3, b]
    haar_edge = np.zeros((128, 128), np.float32)
    for k in range(8):
        for b in range(3):
            haar_edge[2 * k, 8 * b + k] = sign[0, b]
            haar_edge[2 * k + 1, 8 * b + k] = sign[1, b]
            haar_edge[16 + 2 * k, 8 * b + k] = sign[2, b]
            haar_edge[16 + 2 * k + 1, 8 * b + k] = sign[3, b]
    split = np.zeros((256, 256), np.float32)
    for j in range(128):
        split[2 * j, j] = 1.0
        split[2 * j + 1, 128 + j] = 1.0
    out = np.arange(256)
    box = np.zeros((4, 512, 256), np.float32)
    box_edge = np.zeros((4, 3, 256, 256), np.float32)
    for r in range(1, 5):
        inner = (np.abs(out[:, None] - out[None, :]) <= r).astype(np.float32)
        box[r - 1] = np.concatenate([inner, inner])
        for b in range(3):
            side = np.zeros((128, 256), np.float32)
            for k in range(8):
                cell = k - 4 if k < 4 else 252 + k
                side[8 * b + k] = np.abs(cell - out) <= r
            box_edge[r - 1, b] = np.concatenate([side, side])
    join = np.concatenate([split.T] * 3)
    fold = np.zeros((256, 128), np.float32)
    fold[np.arange(256), np.arange(256) // HR] = 1.0
    fold = np.concatenate([fold] * 3)
    every = (perm, edge, haar, haar_edge, split, join, fold, box, box_edge)
    return [jnp.asarray(c, BF16) for c in every]


def dot(a, b):
    return jnp.dot(a, b, preferred_element_type=F32)


def hi_lo(x):
    hi = x.astype(BF16)
    lo = (x - hi.astype(F32)).astype(BF16)
    return hi, lo


def pack_kernel(x_ref, perm_ref, edge_ref, out_ref, y_ref):
    perm = perm_ref[...]
    for c in range(16):
        x = x_ref[:, :, 256 * c : 256 * c + 256].reshape(256, 256)
        y = dot(perm, x).astype(BF16)
        y_ref[c] = y
        d, ct = divmod(c, 2)
        for tb in range(2):
            lane = ct * 512 + tb * 256
            out_ref[d, :, :, lane : lane + 256] = y[tb * 128 : tb * 128 + 128].reshape(HR, OWN, 256)
    for d in range(PH):
        side = jnp.zeros((128, 128), F32)
        for tb in range(2):
            if d > 0:
                side += dot(y_ref[2 * d - 1, pl.ds(tb * 128, 128), :], edge_ref[tb, 0])
            if d < PH - 1:
                side += dot(y_ref[2 * d + 2, pl.ds(tb * 128, 128), :], edge_ref[tb, 1])
        out_ref[d, :, :, 1024:1152] = side.astype(BF16).reshape(HR, OWN, 128)


def packed(photos, perm, edge):
    return pl.pallas_call(
        pack_kernel,
        out_shape=jax.ShapeDtypeStruct((PH, HR, OWN, LANES), BF16),
        in_specs=[pl.BlockSpec(memory_space=pltpu.VMEM)] * 3,
        out_specs=pl.BlockSpec(memory_space=pltpu.VMEM),
        scratch_shapes=[pltpu.VMEM((16, 256, 256), BF16)],
        compiler_params=pltpu.CompilerParams(vmem_limit_bytes=VMEM_LIMIT),
        name="pack",
    )(photos, perm, edge)


def chunk(s, x_ref, ids_ref, consts, scratch):
    haar_ref, haar_edge_ref, split_ref, _, _, box_ref, box_edge_ref = consts
    sq_ref, eq_ref, band_ref, lhs_ref, edge_ref, sum_ref, side_ref, px_ref, data_ref, acc_ref = scratch

    rows = 2 * HR
    for ct in range(2):
        x = x_ref[s, :, :, 512 * ct : 512 * ct + 512].reshape(rows * OWN, 512)
        got = dot(x, haar_ref[...])
        for b in range(3):
            one = got[:, 128 * b : 128 * b + 128].reshape(rows, OWN, 128)
            band_ref[b, :, :, 128 * ct : 128 * ct + 128] = one[4 : 4 + HR]
            sq_ref[b, :, :, 128 * ct : 128 * ct + 128] = one * one
        for tb in range(2):
            lane = 512 * ct + 256 * tb
            x = x_ref[s, pl.ds(4, HR), :, lane : lane + 256].reshape(HR * OWN, 256)
            got = dot(x, split_ref[...])
            for odd in range(2):
                px_ref[2 * tb + odd, :, :, 128 * ct : 128 * ct + 128] = got[
                    :, 128 * odd : 128 * odd + 128
                ].reshape(HR, OWN, 128)
    x = x_ref[s, :, :, 1024:1152].reshape(rows * OWN, 128)
    one = dot(x, haar_edge_ref[...]).reshape(rows, OWN, 128)
    eq_ref[...] = one * one

    def sums(i, _):
        row = eq_ref[i + 4]
        for r in range(1, 5):
            row = row + eq_ref[i + 4 - r] + eq_ref[i + 4 + r]
            hi, lo = hi_lo(row)
            edge_ref[r - 1, i, :, 0:128] = hi
            edge_ref[r - 1, i, :, 128:256] = lo
        for b in range(3):
            row = sq_ref[b, i + 4]
            for r in range(1, 5):
                row = row + sq_ref[b, i + 4 - r] + sq_ref[b, i + 4 + r]
                hi, lo = hi_lo(row)
                lhs_ref[r - 1, b, i, :, 0:256] = hi
                lhs_ref[r - 1, b, i, :, 256:512] = lo
        return 0

    lax.fori_loop(0, HR, sums, 0)

    for r in range(4):
        got = dot(lhs_ref[r].reshape(3 * HR * OWN, 512), box_ref[r])
        sum_ref[r] = got.reshape(3, HR, OWN, 256)
        for b in range(3):
            got = dot(edge_ref[r].reshape(HR * OWN, 256), box_edge_ref[r, b])
            side_ref[r, b] = got.reshape(HR, OWN, 256)

    def residual(i, _):
        res = []
        for b in range(3):
            var = None
            for r in range(4):
                mean = (sum_ref[r, b, i] + side_ref[r, b, i]) * (1.0 / (2 * r + 3) ** 2)
                var = mean if var is None else jnp.minimum(var, mean)
            gain = NOISE_POWER / jnp.maximum(var, NOISE_POWER)
            res.append(band_ref[b, i] * gain * 0.5)
        hz, vt, dg = res
        plus, minus = hz + vt, hz - vt
        noise = (plus + dg, minus - dg, -minus - dg, dg - plus)
        at = pl.multiple_of(i * OWN, OWN)
        for j in range(4):
            x = px_ref[j, i]
            for part, value in enumerate((noise[j].astype(BF16).astype(F32) * x, x * x)):
                hi, lo = hi_lo(value)
                data_ref[2 * j + part, pl.ds(at, OWN), :] = hi
                data_ref[2 * j + part, pl.ds(HR * OWN + at, OWN), :] = lo
        return 0

    lax.fori_loop(0, HR, residual, 0)

    ids = ids_ref[s, 0:1, :]
    row = lax.broadcasted_iota(jnp.int32, (256, 128), 0)
    col = lax.broadcasted_iota(jnp.int32, (256, 128), 1)
    same = (row // HR == ids) & (lax.rem(row, HR) == col // OWN)
    pick = jnp.where(same, 1.0, 0.0).astype(BF16)
    pick = jnp.concatenate([pick, pick], axis=1)
    for j in range(8):
        acc_ref[j] += dot(pick, data_ref[j])


def three(x):
    hi = x.astype(BF16)
    rest = x - hi.astype(F32)
    mid = rest.astype(BF16)
    low = (rest - mid.astype(F32)).astype(BF16)
    return jnp.concatenate([hi, mid, low], axis=1)


def finish(acc_ref, consts, rows_ref, fp_ref, sums_ref):
    _, _, _, join_ref, fold_ref, _, _ = consts
    planes = [acc_ref[2 * j] / acc_ref[2 * j + 1] for j in range(4)]
    for tb in range(2):
        for ct in range(2):
            pair = [planes[2 * tb + odd][:, 128 * ct : 128 * ct + 128] for odd in range(2)]
            got = dot(three(jnp.concatenate(pair, axis=1)), join_ref[...])
            for part in range(2):
                one = got[:, 128 * part : 128 * part + 128].reshape(CAMS, HR, 128)
                rows_ref[2 * ct + part, :, pl.ds(tb, HR, stride=2), :] = one
    for part in range(4):
        fp_ref[:, :, 128 * part : 128 * part + 128] = rows_ref[part]

    gram = jnp.zeros((256, 256), F32)
    for plane in planes:
        hi, lo = hi_lo(plane)
        left = jnp.concatenate([hi, hi, lo], axis=1)
        right = jnp.concatenate([hi, lo, hi], axis=1)
        gram += lax.dot_general(left, right, (((1,), (1,)), ((), ())), preferred_element_type=F32)
    row = lax.broadcasted_iota(jnp.int32, (256, 256), 0)
    col = lax.broadcasted_iota(jnp.int32, (256, 256), 1)
    gram = jnp.where(lax.rem(row, HR) == lax.rem(col, HR), gram, 0.0)
    gram = gram.reshape(CAMS, HR, 256).sum(axis=1)
    gram = dot(three(gram), fold_ref[...])
    total = planes[0] + planes[1] + planes[2] + planes[3]
    total = total.reshape(CAMS, HR, 256).sum(axis=1).sum(axis=1, keepdims=True)
    lane = lax.broadcasted_iota(jnp.int32, (CAMS, 128), 1)
    sums_ref[...] = jnp.where(lane == CAMS, total, gram)


N_CONST = 7


def fused_kernel(ext_ref, idr_ref, *rest):
    const_hbm, rest = rest[:N_CONST], rest[N_CONST:]
    fp_ref, sums_ref, x_ref, ids_ref, rows_ref = rest[:5]
    consts, rest = rest[5 : 5 + N_CONST], rest[5 + N_CONST :]
    scratch, rest = rest[:10], rest[10:]
    acc_ref = scratch[-1]
    (const_sem, own_sem, send_sem, recv_sem, isend_sem, irecv_sem,
     up_send, up_recv, dn_send, dn_recv) = rest
    me = lax.axis_index("photo")
    t = lax.axis_index("tile")

    def loads():
        return [
            pltpu.make_async_copy(a, b, const_sem.at[n])
            for n, (a, b) in enumerate(zip(const_hbm, consts))
        ]

    for copy in loads():
        copy.start()

    barrier = pltpu.get_barrier_semaphore()
    for k in range(1, PH):
        peer = lax.rem(me + k, PH)
        pl.semaphore_signal(barrier, inc=1, device_id={"photo": peer}, device_id_type=MESH)
    for k in (1, TI - 1):
        pl.semaphore_signal(
            barrier, inc=1, device_id={"tile": lax.rem(t + k, TI)}, device_id_type=MESH
        )
    pl.semaphore_wait(barrier, PH + 1)

    def a2a(k):
        peer = lax.rem(me + k, PH)
        return pltpu.make_async_remote_copy(
            src_ref=ext_ref.at[peer], dst_ref=x_ref.at[me, pl.ds(4, HR)],
            send_sem=send_sem.at[k], recv_sem=recv_sem.at[k],
            device_id={"photo": peer}, device_id_type=MESH,
        )

    def idc(k):
        peer = lax.rem(me + k, PH)
        return pltpu.make_async_remote_copy(
            src_ref=idr_ref, dst_ref=ids_ref.at[me],
            send_sem=isend_sem.at[k], recv_sem=irecv_sem.at[k],
            device_id={"photo": peer}, device_id_type=MESH,
        )

    def up(k, src, s):
        return pltpu.make_async_remote_copy(
            src_ref=src, dst_ref=x_ref.at[s, pl.ds(12, 4)],
            send_sem=up_send.at[k], recv_sem=up_recv.at[k],
            device_id={"tile": t - 1}, device_id_type=MESH,
        )

    def down(k, src, s):
        return pltpu.make_async_remote_copy(
            src_ref=src, dst_ref=x_ref.at[s, pl.ds(0, 4)],
            send_sem=dn_send.at[k], recv_sem=dn_recv.at[k],
            device_id={"tile": t + 1}, device_id_type=MESH,
        )

    def pass_on(k, first, last, s):
        @pl.when(t > 0)
        def _():
            up(k, first, s).start()

        @pl.when(t < TI - 1)
        def _():
            down(k, last, s).start()

    for k in range(1, PH):
        a2a(k).start()
    pass_on(0, ext_ref.at[me, pl.ds(0, 4)], ext_ref.at[me, pl.ds(4, 4)], me)
    for k in range(1, PH):
        idc(k).start()
    own = pltpu.make_async_copy(ext_ref.at[me], x_ref.at[me, pl.ds(4, HR)], own_sem.at[0])
    own.start()
    own_id = pltpu.make_async_copy(idr_ref, ids_ref.at[me], own_sem.at[1])
    own_id.start()

    @pl.when(t == 0)
    def _():
        x_ref[:, pl.ds(0, 4)] = jnp.zeros((PH, 4, OWN, LANES), BF16)

    @pl.when(t == TI - 1)
    def _():
        x_ref[:, pl.ds(12, 4)] = jnp.zeros((PH, 4, OWN, LANES), BF16)

    acc_ref[...] = jnp.zeros(acc_ref.shape, F32)
    own.wait()
    own_id.wait()
    for copy in loads():
        copy.wait()

    def step(k, _):
        s = lax.rem(me + PH - k, PH)

        @pl.when(k < PH - 1)
        def _():
            after = lax.rem(me + PH - 1 - k, PH)
            a2a(k + 1).wait_recv()
            idc(k + 1).wait_recv()
            pass_on(k + 1, x_ref.at[after, pl.ds(4, 4)], x_ref.at[after, pl.ds(8, 4)], after)

        @pl.when(t > 0)
        def _():
            down(k, x_ref.at[s, pl.ds(8, 4)], s).wait_recv()

        @pl.when(t < TI - 1)
        def _():
            up(k, x_ref.at[s, pl.ds(4, 4)], s).wait_recv()

        chunk(s, x_ref, ids_ref, consts, scratch)
        return 0

    lax.fori_loop(0, PH, step, 0)
    finish(acc_ref, consts, rows_ref, fp_ref, sums_ref)

    for k in range(1, PH):
        a2a(k).wait_send()
        idc(k).wait_send()
    for k in range(PH):
        s = lax.rem(me + PH - k, PH)

        @pl.when(t > 0)
        def _():
            up(k, x_ref.at[s, pl.ds(4, 4)], s).wait_send()

        @pl.when(t < TI - 1)
        def _():
            down(k, x_ref.at[s, pl.ds(8, 4)], s).wait_send()


SCRATCH = [
    ((3, 2 * HR, OWN, 256), F32),
    ((2 * HR, OWN, 128), F32),
    ((3, HR, OWN, 256), F32),
    ((4, 3, HR, OWN, 512), BF16),
    ((4, HR, OWN, 256), BF16),
    ((4, 3, HR, OWN, 256), F32),
    ((4, 3, HR, OWN, 256), F32),
    ((4, HR, OWN, 256), F32),
    ((8, 256, 256), BF16),
    ((8, 256, 256), F32),
]


def fused(ext, idr, consts):
    vm = pl.BlockSpec(memory_space=pltpu.VMEM)
    anywhere = pl.BlockSpec(memory_space=pl.ANY)
    dma = pltpu.SemaphoreType.DMA
    return pl.pallas_call(
        fused_kernel,
        out_shape=(
            jax.ShapeDtypeStruct((CAMS, 16, 512), F32),
            jax.ShapeDtypeStruct((CAMS, 128), F32),
        ),
        in_specs=[anywhere] * (2 + N_CONST),
        out_specs=(vm, vm),
        scratch_shapes=[
            pltpu.VMEM((PH, 2 * HR, OWN, LANES), BF16),
            pltpu.VMEM((PH, 8, 128), jnp.int32),
            pltpu.VMEM((4, CAMS, 16, 128), F32),
        ]
        + [pltpu.VMEM(c.shape, c.dtype) for c in consts]
        + [pltpu.VMEM(s, d) for s, d in SCRATCH]
        + [dma((N_CONST,)), dma((2,))]
        + [dma((PH,))] * 8,
        compiler_params=pltpu.CompilerParams(
            collective_id=0, has_side_effects=True, vmem_limit_bytes=VMEM_LIMIT
        ),
        name="fused",
    )(ext, idr, *consts)


def correlated(total):
    pixels = float(256 * 4096)
    row = lax.broadcasted_iota(jnp.int32, total.shape, 0)
    lane = lax.broadcasted_iota(jnp.int32, total.shape, 1)
    average = total[:, CAMS : CAMS + 1] / pixels
    across = jnp.sum(jnp.where(row == lane, average, 0.0), axis=0, keepdims=True)
    covar = total / pixels - average * across
    own = jnp.where(row == lane, covar, 0.0)
    down = jnp.sum(own, axis=1, keepdims=True) + VAR_EPS
    along = jnp.sum(own, axis=0, keepdims=True) + VAR_EPS
    return covar / jnp.sqrt(down * along)


def allsum_kernel(x_ref, o_ref, a_ref, m_ref, b_ref, as_sem, ar_sem, bs_sem, br_sem):
    me = lax.axis_index("photo")
    t = lax.axis_index("tile")
    barrier = pltpu.get_barrier_semaphore()
    for k in range(1, PH):
        pl.semaphore_signal(
            barrier, inc=1, device_id={"photo": lax.rem(me + k, PH)}, device_id_type=MESH
        )
    for k in range(1, TI):
        pl.semaphore_signal(
            barrier, inc=1, device_id={"tile": lax.rem(t + k, TI)}, device_id_type=MESH
        )
    pl.semaphore_wait(barrier, PH + TI - 2)

    def first(k):
        return pltpu.make_async_remote_copy(
            src_ref=x_ref, dst_ref=a_ref.at[k - 1], send_sem=as_sem.at[k - 1],
            recv_sem=ar_sem.at[k - 1],
            device_id={"photo": lax.rem(me + k, PH)}, device_id_type=MESH,
        )

    def second(k):
        return pltpu.make_async_remote_copy(
            src_ref=m_ref, dst_ref=b_ref.at[k - 1], send_sem=bs_sem.at[k - 1],
            recv_sem=br_sem.at[k - 1],
            device_id={"tile": lax.rem(t + k, TI)}, device_id_type=MESH,
        )

    for k in range(1, PH):
        first(k).start()
    for k in range(1, PH):
        first(k).wait_recv()
    total = jnp.zeros(x_ref.shape, F32)
    for s in range(PH):
        k = lax.rem(me + PH - s, PH)
        other = a_ref[jnp.maximum(k - 1, 0)]
        total += jnp.where(k == 0, x_ref[...], other)
    m_ref[...] = total
    for k in range(1, TI):
        second(k).start()
    for k in range(1, TI):
        second(k).wait_recv()
    total = jnp.zeros(x_ref.shape, F32)
    for s in range(TI):
        k = lax.rem(t + TI - s, TI)
        other = b_ref[jnp.maximum(k - 1, 0)]
        total += jnp.where(k == 0, m_ref[...], other)
    o_ref[...] = correlated(total)[:, :CAMS]
    for k in range(1, PH):
        first(k).wait_send()
    for k in range(1, TI):
        second(k).wait_send()


def allsum(x):
    vm = pl.BlockSpec(memory_space=pltpu.VMEM)
    dma = pltpu.SemaphoreType.DMA
    return pl.pallas_call(
        allsum_kernel,
        out_shape=jax.ShapeDtypeStruct((CAMS, CAMS), F32),
        in_specs=[vm],
        out_specs=vm,
        scratch_shapes=[
            pltpu.VMEM((PH - 1,) + x.shape, F32),
            pltpu.VMEM(x.shape, F32),
            pltpu.VMEM((TI - 1,) + x.shape, F32),
            dma((PH - 1,)), dma((PH - 1,)), dma((TI - 1,)), dma((TI - 1,)),
        ],
        compiler_params=pltpu.CompilerParams(collective_id=1, has_side_effects=True),
        name="allsum",
    )(x)


def on_device(photos, camera_id):
    perm, edge, *consts = constants()
    ext = packed(photos, perm, edge)
    idr = jnp.broadcast_to(camera_id[None, None, :], (8, HR, OWN))
    fingerprints, sums = fused(ext, idr.reshape(8, 128), consts)
    return (fingerprints, allsum(sums))


def solution(mesh):
    return jax.shard_map(
        on_device,
        mesh=mesh,
        in_specs=(P("photo", "tile", None), P("photo")),
        out_specs=(P(None, "tile", "photo"), P()),
        check_vma=False,
    )
```

time: 112 us -> 95.6 us (0.85)
  Pallas kernels: 97.4 us -> 90.4 us
  other arithmetic: 6.59 us -> 0 us
  matrix products: 4.33 us -> 0 us
  local copies, waits for them, and re-layouts: 2.22 us -> 4.26 us
    pallas_call x3 -> x2, Pallas kernels: 93.1 us -> 86.1 us  [the longest x1 61.7 us: fused(): pl.pallas_call(fused_kernel, out_shape=(jax.ShapeDtypeStruct((CAMS, 16, 5...]
    dot_general x1 -> x0, matrix products: 4.33 us -> none  [on_device(): jnp.dot(flat, flat.T, precision=lax.Precision.HIGHEST, preferred_element_...]
    unnamed x4, local copies, waits for them, and re-layouts: 0.6 us -> 2.92 us
    div x2 -> x0, other arithmetic: 2.3 us -> none  [the longest x1 1.4 us: on_device(): correlation = covar / jnp.sqrt(spread[:, None] * spread[None, :])]
    another operation x3 -> x0, other arithmetic: 1.92 us -> none
    reduce_sum x1 -> x0, other arithmetic: 1.55 us -> none  [on_device(): totals_local = jnp.sum(flat, axis=1)]
where the time goes in v2:
time: 95.6 us; the launch traced here: 95.3 us
  Pallas kernels  90.4 us (95%)
  local copies, waits for them, and re-layouts  4.26 us (4%)
    pallas_call x1, Pallas kernels, fused(): pl.pallas_call(fused_kernel, out_shape=(jax.ShapeDtypeStruct((CAMS, 16, 5...  61.7 us
    pallas_call x1, Pallas kernels, allsum(): pl.pallas_call(allsum_kernel, out_shape=jax.ShapeDtypeStruct((CAMS, CAMS)...  24.4 us
    pallas_call x1, Pallas kernels, packed(): pl.pallas_call(pack_kernel, out_shape=jax.ShapeDtypeStruct((PH, HR, OWN,...  4.29 us
    unnamed x4, local copies, waits for them, and re-layouts  2.92 us

profile of v2, /device:TPU:1, one launch (start us, length us, event | category | flops | bytes accessed | tf_op | source)
XLA Modules:
  0.0 95.3 jit_solution(12415547353505603320)
XLA Ops:
  0.6 0.7 broadcast_in_dim.10
  1.3 0.1 broadcast_in_dim.11
  1.4 0.6 broadcast_in_dim.12.idr_ref
  2.0 4.3 %pack.1.ext_ref = bf16[8,8,16,1152]{3,2,1,0:T(8,128)(2,1)} custom-call(bf16[16,16,4096]{2,1,0:T(8,128)(2,1)} %x_ref.1, bf16[256,256]{1,0:T(8,128)(2,1)} %constant.18.clone.perm_ref, bf16[2,2,256,128]{3,2,1,0:T(8,128)(2,1)} %constant.19.clone.edge_ref), custom_call_target="tpu_custom_call" | custom-call | tf_op jit(solution)/shard_map/pack/pallas_call | solution.py:108
  6.3 61.7 %fused.1 = (f32[32,16,512]{2,1,0:T(8,128)}, f32[32,128]{1,0:T(8,128)}) custom-call(bf16[8,8,16,1152]{3,2,1,0:T(8,128)(2,1)} %pack.1.ext_ref, s32[8,128]{1,0:T(8,128)} %broadcast_in_dim.12.idr_ref, bf16[512,384]{1,0:T(8,128)(2,1)} %constant.20.clone.rest_0_, bf16[128,128]{1,0:T(8,128)(2,1)} %constant.21.clone.rest_1_, ...), custom_call_target="tpu_custom_call" | custom-call | tf_op jit(solution)/shard_map/fused/pallas_call | solution.py:392
  68.0 24.4 %allsum.1 = f32[32,32]{1,0:T(8,128)} custom-call(f32[32,128]{1,0:T(8,128)} %get-tuple-element.5.x_ref), custom_call_target="tpu_custom_call" | custom-call | tf_op jit(solution)/shard_map/allsum/pallas_call | solution.py:486
  92.4 0.0 copy-start
  92.4 2.3 %copy.15 = f32[32,16,512]{2,1,0:T(8,128)} copy(f32[32,16,512]{2,1,0:T(8,128)} %get-tuple-element.8) | data formatting | bytes 2097152
  94.7 0.0 copy-done
  94.7 0.6 copy.16
Async XLA Ops:
  92.4 2.3 %copy-start = (f32[32,32]{1,0:T(8,128)S(1)}, f32[32,32]{1,0:T(8,128)}, u32[]{:S(2)}) copy-start(f32[32,32]{1,0:T(8,128)} %allsum.1) | copy-start | bytes 12292

commit v3 on v2

v3 whole, which is shorter than its diff:
```python
import functools

import jax
import jax.numpy as jnp
import numpy as np
from jax import lax
from jax.experimental import pallas as pl
from jax.experimental.pallas import tpu as pltpu
from jax.sharding import PartitionSpec as P

MESH = pl.DeviceIdType.MESH
F32 = jnp.float32
BF16 = jnp.bfloat16

CAMS = 32
NOISE_POWER = 1.0
VAR_EPS = 1e-06

PH = 8
TI = 16
OWN = 16
HR = 8
LANES = 1024
VMEM_LIMIT = 60 * 1024 * 1024


def constants():
    perm = np.zeros((256, 256), np.float32)
    for tb in range(2):
        for i in range(HR):
            for p in range(OWN):
                perm[(tb * HR + i) * OWN + p, p * 16 + 2 * i + tb] = 1.0
    edge = np.zeros((8, 256, 128), np.float32)
    for jt in range(8):
        for k in range(8):
            edge[jt, 120 + k, 16 * jt + k] = 1.0
            edge[jt, 128 + k, 16 * jt + 8 + k] = 1.0
    sign = np.array([[1, 1, 1], [1, -1, -1], [-1, 1, -1], [-1, -1, 1]], np.float32) * 0.5
    haar = np.zeros((512, 384), np.float32)
    for j in range(128):
        for b in range(3):
            haar[2 * j, 128 * b + j] = sign[0, b]
            haar[2 * j + 1, 128 * b + j] = sign[1, b]
            haar[256 + 2 * j, 128 * b + j] = sign[2, b]
            haar[256 + 2 * j + 1, 128 * b + j] = sign[3, b]
    haar_edge = np.zeros((128, 512), np.float32)
    for j in range(4):
        for k in range(8):
            for b in range(3):
                for n in range(4):
                    at = 32 * j + 16 * (n // 2) + 2 * k + n % 2
                    haar_edge[at, 128 * j + 8 * b + k] = sign[n, b]
    split = np.zeros((256, 256), np.float32)
    for j in range(128):
        split[2 * j, j] = 1.0
        split[2 * j + 1, 128 + j] = 1.0
    out = np.arange(256)
    box = np.zeros((4, 512, 256), np.float32)
    box_edge = np.zeros((4, 3, 256, 256), np.float32)
    for r in range(1, 5):
        inner = (np.abs(out[:, None] - out[None, :]) <= r).astype(np.float32)
        box[r - 1] = np.concatenate([inner, inner])
        for b in range(3):
            side = np.zeros((128, 256), np.float32)
            for k in range(8):
                cell = k - 4 if k < 4 else 252 + k
                side[8 * b + k] = np.abs(cell - out) <= r
            box_edge[r - 1, b] = np.concatenate([side, side])
    join = np.concatenate([split.T] * 3)
    fold = np.zeros((256, 128), np.float32)
    fold[np.arange(256), np.arange(256) // HR] = 1.0
    fold = np.concatenate([fold] * 3)
    every = (perm, edge, haar, haar_edge, split, join, fold, box, box_edge)
    return [jnp.asarray(c, BF16) for c in every]


def dot(a, b):
    return jnp.dot(a, b, preferred_element_type=F32)


def hi_lo(x):
    hi = x.astype(BF16)
    lo = (x - hi.astype(F32)).astype(BF16)
    return hi, lo


def chunk(s, x_ref, e_ref, consts, scratch):
    haar_ref, haar_edge_ref, split_ref, _, _, box_ref, box_edge_ref = consts[2:]
    sq_ref, eq_ref, band_ref, lhs_ref, edge_ref, sum_ref, side_ref, px_ref, data_ref, acc_ref = scratch

    rows = 2 * HR
    for ct in range(2):
        x = x_ref[s, :, :, 512 * ct : 512 * ct + 512].reshape(rows * OWN, 512)
        got = dot(x, haar_ref[...])
        for b in range(3):
            one = got[:, 128 * b : 128 * b + 128].reshape(rows, OWN, 128)
            band_ref[b, :, :, 128 * ct : 128 * ct + 128] = one[4 : 4 + HR]
            sq_ref[b, :, :, 128 * ct : 128 * ct + 128] = one * one
        for tb in range(2):
            lane = 512 * ct + 256 * tb
            x = x_ref[s, pl.ds(4, HR), :, lane : lane + 256].reshape(HR * OWN, 256)
            got = dot(x, split_ref[...])
            for odd in range(2):
                px_ref[2 * tb + odd, :, :, 128 * ct : 128 * ct + 128] = got[
                    :, 128 * odd : 128 * odd + 128
                ].reshape(HR, OWN, 128)
    x = jnp.concatenate([e_ref[s, n] for n in (0, 1, 2, 4)])
    one = dot(x, haar_edge_ref[...])
    for n in range(rows):
        g, j = divmod(n, 4)
        part = one[OWN * g : OWN * g + OWN, 128 * j : 128 * j + 128]
        eq_ref[n] = part * part

    def sums(i, _):
        row = eq_ref[i + 4]
        for r in range(1, 5):
            row = row + eq_ref[i + 4 - r] + eq_ref[i + 4 + r]
            hi, lo = hi_lo(row)
            edge_ref[r - 1, i, :, 0:128] = hi
            edge_ref[r - 1, i, :, 128:256] = lo
        for b in range(3):
            row = sq_ref[b, i + 4]
            for r in range(1, 5):
                row = row + sq_ref[b, i + 4 - r] + sq_ref[b, i + 4 + r]
                hi, lo = hi_lo(row)
                lhs_ref[r - 1, b, i, :, 0:256] = hi
                lhs_ref[r - 1, b, i, :, 256:512] = lo
        return 0

    lax.fori_loop(0, HR, sums, 0)

    for r in range(4):
        got = dot(lhs_ref[r].reshape(3 * HR * OWN, 512), box_ref[r])
        sum_ref[r] = got.reshape(3, HR, OWN, 256)
        for b in range(3):
            got = dot(edge_ref[r].reshape(HR * OWN, 256), box_edge_ref[r, b])
            side_ref[r, b] = got.reshape(HR, OWN, 256)

    def residual(i, _):
        res = []
        for b in range(3):
            var = None
            for r in range(4):
                mean = (sum_ref[r, b, i] + side_ref[r, b, i]) * (1.0 / (2 * r + 3) ** 2)
                var = mean if var is None else jnp.minimum(var, mean)
            gain = NOISE_POWER / jnp.maximum(var, NOISE_POWER)
            res.append(band_ref[b, i] * gain * 0.5)
        hz, vt, dg = res
        plus, minus = hz + vt, hz - vt
        noise = (plus + dg, minus - dg, -minus - dg, dg - plus)
        at = pl.multiple_of(i * OWN, OWN)
        for j in range(4):
            x = px_ref[j, i]
            for part, value in enumerate((noise[j].astype(BF16).astype(F32) * x, x * x)):
                hi, lo = hi_lo(value)
                data_ref[2 * j + part, pl.ds(at, OWN), :] = hi
                data_ref[2 * j + part, pl.ds(HR * OWN + at, OWN), :] = lo
        return 0

    lax.fori_loop(0, HR, residual, 0)

    ids = e_ref[s, 3].astype(F32)[0:1, :]
    row = lax.broadcasted_iota(jnp.int32, (256, 128), 0)
    col = lax.broadcasted_iota(jnp.int32, (256, 128), 1)
    same = ((row // HR).astype(F32) == ids) & (lax.rem(row, HR) == col // OWN)
    pick = jnp.where(same, 1.0, 0.0).astype(BF16)
    pick = jnp.concatenate([pick, pick], axis=1)
    for j in range(8):
        acc_ref[j] += dot(pick, data_ref[j])


def three(x):
    hi = x.astype(BF16)
    rest = x - hi.astype(F32)
    mid = rest.astype(BF16)
    low = (rest - mid.astype(F32)).astype(BF16)
    return jnp.concatenate([hi, mid, low], axis=1)


def total_gram(acc_ref, fold_ref):
    planes = [acc_ref[2 * j] / acc_ref[2 * j + 1] for j in range(4)]
    gram = jnp.zeros((256, 256), F32)
    for plane in planes:
        hi, lo = hi_lo(plane)
        left = jnp.concatenate([hi, hi, lo], axis=1)
        right = jnp.concatenate([hi, lo, hi], axis=1)
        gram += lax.dot_general(left, right, (((1,), (1,)), ((), ())), preferred_element_type=F32)
    row = lax.broadcasted_iota(jnp.int32, (256, 256), 0)
    col = lax.broadcasted_iota(jnp.int32, (256, 256), 1)
    gram = jnp.where(lax.rem(row, HR) == lax.rem(col, HR), gram, 0.0)
    gram = gram.reshape(CAMS, HR, 256).sum(axis=1)
    gram = dot(three(gram), fold_ref[...])
    total = planes[0] + planes[1] + planes[2] + planes[3]
    total = total.reshape(CAMS, HR, 256).sum(axis=1).sum(axis=1, keepdims=True)
    lane = lax.broadcasted_iota(jnp.int32, (8, 128), 1)
    upper, lower = jnp.zeros((8, 128), F32), jnp.zeros((8, 128), F32)
    for q in range(4):
        part = gram[8 * q : 8 * q + 8]
        if q:
            part = pltpu.roll(part, 32 * q, 1)
        upper = jnp.where(lane // 32 == q, part, upper)
        lower = jnp.where(lane == q, total[8 * q : 8 * q + 8], lower)
    return planes, jnp.concatenate([upper, lower])


def correlated(sums):
    upper, lower = sums[0:8], sums[8:16]
    gram = jnp.concatenate([upper] + [pltpu.roll(upper, 128 - 32 * q, 1) for q in range(1, 4)])
    total = jnp.concatenate([lower[:, q : q + 1] for q in range(4)])
    pixels = float(256 * 4096)
    row = lax.broadcasted_iota(jnp.int32, gram.shape, 0)
    lane = lax.broadcasted_iota(jnp.int32, gram.shape, 1)
    average = total / pixels
    across = jnp.sum(jnp.where(row == lane, average, 0.0), axis=0, keepdims=True)
    covar = gram / pixels - average * across
    own = jnp.where(row == lane, covar, 0.0)
    down = jnp.sum(own, axis=1, keepdims=True) + VAR_EPS
    along = jnp.sum(own, axis=0, keepdims=True) + VAR_EPS
    return (covar / jnp.sqrt(down * along))[:, :CAMS]


def join(planes, join_ref, rows_ref):
    for tb in range(2):
        for ct in range(2):
            pair = [planes[2 * tb + odd][:, 128 * ct : 128 * ct + 128] for odd in range(2)]
            got = dot(three(jnp.concatenate(pair, axis=1)), join_ref[...])
            for part in range(2):
                one = got[:, 128 * part : 128 * part + 128].reshape(CAMS, HR, 128)
                rows_ref[2 * ct + part, :, pl.ds(tb, HR, stride=2), :] = one


def pack(photo_ref, cid_ref, perm_ref, edge_ref, block_ref, side_ref, beside_ref):
    beside_ref[:, 1, :, :, 0:128] = jnp.zeros((8, 2, OWN, 128), BF16)
    beside_ref[:, PH, :, :, 128:256] = jnp.zeros((8, 2, OWN, 128), BF16)

    def block(d, _):
        for ct in range(2):
            lane = pl.multiple_of(512 * d + 256 * ct, 256)
            x = photo_ref[:, :, pl.ds(lane, 256)].reshape(256, 256)
            y = dot(perm_ref[...], x).astype(BF16).reshape(2, HR, OWN, 256)
            for tb in range(2):
                lane = ct * 512 + tb * 256
                block_ref[d, :, :, lane : lane + 256] = y[tb]
                for i in range(HR):
                    g, j = divmod(i, 4)
                    if ct == 0:
                        beside_ref[2 * j + tb, d, g, :, 128:256] = y[tb, i, :, 0:128]
                    else:
                        beside_ref[2 * j + tb, d + 2, g, :, 0:128] = y[tb, i, :, 128:256]
        return 0

    lax.fori_loop(0, PH, block, 0)
    side = jnp.zeros((256, 128), F32)
    for jt in range(8):
        side += dot(beside_ref[jt, pl.ds(1, PH)].reshape(256, 256), edge_ref[jt])
    side_ref[:, pl.ds(0, 2)] = side.astype(BF16).reshape(PH, 2, OWN, 128)
    lane = lax.broadcasted_iota(jnp.int32, (OWN, 128), 1)
    ids = jnp.zeros((OWN, 128), jnp.int32)
    for n in range(OWN):
        ids = jnp.where(lax.rem(lane, OWN) == n, cid_ref[n], ids)
    ids = ids.astype(F32).astype(BF16)
    for d in range(PH):
        side_ref[d, 2] = ids


N_CONST = 9


def fused_kernel(photo_ref, cid_ref, *rest):
    const_hbm, rest = rest[:N_CONST], rest[N_CONST:]
    fp_ref, corr_ref, block_ref, side_ref, beside_ref, x_ref, e_ref, rows_ref, a_ref, b_ref = rest[:10]
    consts, rest = rest[10 : 10 + N_CONST], rest[10 + N_CONST :]
    scratch, rest = rest[:10], rest[10:]
    acc_ref = scratch[-1]
    (const_sem, own_sem, send_sem, recv_sem, up_send, up_recv, dn_send, dn_recv,
     as_sem, ar_sem, bs_sem, br_sem) = rest
    me = lax.axis_index("photo")
    t = lax.axis_index("tile")

    def load(n):
        return pltpu.make_async_copy(const_hbm[n], consts[n], const_sem.at[n])

    for n in range(N_CONST):
        load(n).start()

    barrier = pltpu.get_barrier_semaphore()
    middle = t * (TI - 1 - t) // 56
    for k in range(1, PH):
        peer = lax.rem(me + k, PH)
        pl.semaphore_signal(barrier, inc=1, device_id={"photo": peer}, device_id_type=MESH)
    for k in range(1, TI):
        pl.semaphore_signal(
            barrier, inc=1, device_id={"tile": lax.rem(t + k, TI)}, device_id_type=MESH
        )

    @pl.when(middle == 1)
    def _():
        for k in range(1, PH):
            where = {"photo": lax.rem(me + k, PH), "tile": TI - 1 - t}
            pl.semaphore_signal(barrier, inc=1, device_id=where, device_id_type=MESH)

    load(0).wait()
    load(1).wait()
    pack(photo_ref, cid_ref, consts[0], consts[1], block_ref, side_ref, beside_ref)
    pl.semaphore_wait(barrier, PH + TI - 2 + (PH - 1) * middle)

    def remote(srcs, dsts, send, recv, k, where):
        return [
            pltpu.make_async_remote_copy(
                src_ref=a, dst_ref=b, send_sem=send.at[n, k], recv_sem=recv.at[n, k],
                device_id=where, device_id_type=MESH,
            )
            for n, (a, b) in enumerate(zip(srcs, dsts))
        ]

    def a2a(k):
        peer = lax.rem(me + k, PH)
        return remote(
            (block_ref.at[peer], side_ref.at[peer]),
            (x_ref.at[me, pl.ds(4, HR)], e_ref.at[me, pl.ds(1, 3)]),
            send_sem, recv_sem, k, {"photo": peer},
        )

    def up(k, srcs, s, where):
        dsts = (x_ref.at[s, pl.ds(12, 4)], e_ref.at[s, 4])
        return remote(srcs, dsts, up_send, up_recv, k, where)

    def down(k, srcs, s, where):
        dsts = (x_ref.at[s, pl.ds(0, 4)], e_ref.at[s, 0])
        return remote(srcs, dsts, dn_send, dn_recv, k, where)

    def held(s, first):
        return (x_ref.at[s, pl.ds(4 if first else 8, 4)], e_ref.at[s, 1 if first else 2])

    def mine(d, first):
        return (block_ref.at[d, pl.ds(0 if first else 4, 4)], side_ref.at[d, 0 if first else 1])

    def each(copies, act):
        for copy in copies:
            getattr(copy, act)()

    for k in range(1, PH):
        each(a2a(k), "start")

    @pl.when(t == TI // 2 - 1)
    def _():
        for k in range(PH):
            peer = lax.rem(me + k, PH)
            each(down(k, mine(peer, False), me, {"photo": peer, "tile": t + 1}), "start")

    @pl.when(t == TI // 2)
    def _():
        for k in range(PH):
            peer = lax.rem(me + k, PH)
            each(up(k, mine(peer, True), me, {"photo": peer, "tile": t - 1}), "start")

    def pass_on(k, source, s):
        @pl.when((t > 0) & (t != TI // 2))
        def _():
            each(up(k, source(s, True), s, {"tile": t - 1}), "start")

        @pl.when((t < TI - 1) & (t != TI // 2 - 1))
        def _():
            each(down(k, source(s, False), s, {"tile": t + 1}), "start")

    pass_on(0, mine, me)
    own = [
        pltpu.make_async_copy(block_ref.at[me], x_ref.at[me, pl.ds(4, HR)], own_sem.at[0]),
        pltpu.make_async_copy(side_ref.at[me], e_ref.at[me, pl.ds(1, 3)], own_sem.at[1]),
    ]
    each(own, "start")

    @pl.when(t == 0)
    def _():
        x_ref[:, pl.ds(0, 4)] = jnp.zeros((PH, 4, OWN, LANES), BF16)
        e_ref[:, 0] = jnp.zeros((PH, OWN, 128), BF16)

    @pl.when(t == TI - 1)
    def _():
        x_ref[:, pl.ds(12, 4)] = jnp.zeros((PH, 4, OWN, LANES), BF16)
        e_ref[:, 4] = jnp.zeros((PH, OWN, 128), BF16)

    acc_ref[...] = jnp.zeros(acc_ref.shape, F32)
    each(own, "wait")
    for n in range(2, N_CONST):
        load(n).wait()

    def step(k, _):
        s = lax.rem(me + PH - k, PH)

        @pl.when(k < PH - 1)
        def _():
            after = lax.rem(me + PH - 1 - k, PH)
            each(a2a(k + 1), "wait_recv")
            pass_on(k + 1, held, after)

        @pl.when(t > 0)
        def _():
            each(down(k, held(s, False), s, {"tile": t - 1}), "wait_recv")

        @pl.when(t < TI - 1)
        def _():
            each(up(k, held(s, True), s, {"tile": t + 1}), "wait_recv")

        chunk(s, x_ref, e_ref, consts, scratch)
        return 0

    lax.fori_loop(0, PH, step, 0)

    def first(k):
        return pltpu.make_async_remote_copy(
            src_ref=a_ref.at[me], dst_ref=a_ref.at[me], send_sem=as_sem.at[k],
            recv_sem=ar_sem.at[k],
            device_id={"photo": lax.rem(me + k, PH)}, device_id_type=MESH,
        )

    def second(k):
        return pltpu.make_async_remote_copy(
            src_ref=b_ref.at[t], dst_ref=b_ref.at[t], send_sem=bs_sem.at[k],
            recv_sem=br_sem.at[k],
            device_id={"tile": lax.rem(t + k, TI)}, device_id_type=MESH,
        )

    planes, sums = total_gram(acc_ref, consts[6])
    a_ref[me] = sums
    for k in range(1, PH):
        first(k).start()
    join(planes, consts[5], rows_ref)
    out = [
        pltpu.make_async_copy(
            rows_ref.at[n], fp_ref.at[:, :, pl.ds(128 * n, 128)], own_sem.at[2 + n]
        )
        for n in range(4)
    ]
    each(out, "start")
    for k in range(1, PH):
        first(k).wait_recv()
    sums = a_ref[0]
    for n in range(1, PH):
        sums += a_ref[n]
    b_ref[t] = sums
    for k in range(1, TI):
        second(k).start()
    for k in range(1, TI):
        second(k).wait_recv()
    sums = b_ref[0]
    for n in range(1, TI):
        sums += b_ref[n]
    corr_ref[...] = correlated(sums)

    each(out, "wait")
    for k in range(1, PH):
        each(a2a(k), "wait_send")
        first(k).wait_send()
    for k in range(1, TI):
        second(k).wait_send()
    for k in range(PH):
        s = lax.rem(me + PH - k, PH)

        @pl.when(t > 0)
        def _():
            each(up(k, held(s, True), s, {"tile": t - 1}), "wait_send")

        @pl.when(t < TI - 1)
        def _():
            each(down(k, held(s, False), s, {"tile": t + 1}), "wait_send")


SCRATCH = [
    ((3, 2 * HR, OWN, 256), F32),
    ((2 * HR, OWN, 128), F32),
    ((3, HR, OWN, 256), F32),
    ((4, 3, HR, OWN, 512), BF16),
    ((4, HR, OWN, 256), BF16),
    ((4, 3, HR, OWN, 256), F32),
    ((4, 3, HR, OWN, 256), F32),
    ((4, HR, OWN, 256), F32),
    ((8, 256, 256), BF16),
    ((8, 256, 256), F32),
]


def fused(photos, camera_id, consts):
    vm = pl.BlockSpec(memory_space=pltpu.VMEM)
    anywhere = pl.BlockSpec(memory_space=pl.ANY)
    dma = pltpu.SemaphoreType.DMA
    return pl.pallas_call(
        fused_kernel,
        out_shape=(
            jax.ShapeDtypeStruct((CAMS, 16, 512), F32),
            jax.ShapeDtypeStruct((CAMS, CAMS), F32),
        ),
        in_specs=[vm, pl.BlockSpec(memory_space=pltpu.SMEM)] + [anywhere] * N_CONST,
        out_specs=(anywhere, vm),
        scratch_shapes=[
            pltpu.VMEM((PH, HR, OWN, LANES), BF16),
            pltpu.VMEM((PH, 3, OWN, 128), BF16),
            pltpu.VMEM((8, PH + 2, 2, OWN, 256), BF16),
            pltpu.VMEM((PH, 2 * HR, OWN, LANES), BF16),
            pltpu.VMEM((PH, 5, OWN, 128), BF16),
            pltpu.VMEM((4, CAMS, 16, 128), F32),
            pltpu.VMEM((PH, 16, 128), F32),
            pltpu.VMEM((TI, 16, 128), F32),
        ]
        + [pltpu.VMEM(c.shape, c.dtype) for c in consts]
        + [pltpu.VMEM(s, d) for s, d in SCRATCH]
        + [dma((N_CONST,)), dma((6,))]
        + [dma((2, PH))] * 6
        + [dma((PH,))] * 2
        + [dma((TI,))] * 2,
        compiler_params=pltpu.CompilerParams(
            collective_id=0, has_side_effects=True, vmem_limit_bytes=VMEM_LIMIT
        ),
        name="fused",
    )(photos, camera_id, *consts)


def on_device(photos, camera_id):
    return fused(photos, camera_id, constants())


def solution(mesh):
    return jax.shard_map(
        on_device,
        mesh=mesh,
        in_specs=(P("photo", "tile", None), P("photo")),
        out_specs=(P(None, "tile", "photo"), P()),
        check_vma=False,
    )
```

time: 95.6 us -> 77.2 us (0.81)
  Pallas kernels: 90.4 us -> 73.5 us
  local copies, waits for them, and re-layouts: 4.26 us -> 2.92 us
    pallas_call x2 -> x0, Pallas kernels: 28.7 us -> none  [the longest x1 24.4 us: allsum(): pl.pallas_call(allsum_kernel, out_shape=jax.ShapeDtypeStruct((CAMS, CAMS)...]
    pallas_call x1, Pallas kernels: 61.7 us -> 73.5 us  [fused(): pl.pallas_call(fused_kernel, out_shape=(jax.ShapeDtypeStruct((CAMS, 16, 5...]
    broadcast_in_dim x3 -> x0, local copies, waits for them, and re-layouts: 1.34 us -> none  [on_device(): idr = jnp.broadcast_to(camera_id[None, None, :], (8, HR, OWN))]
where the time goes in v3:
time: 77.2 us; the launch traced here: 77.1 us
  Pallas kernels  73.5 us (95%)
  local copies, waits for them, and re-layouts  2.92 us (4%)
    pallas_call x1, Pallas kernels, fused(): pl.pallas_call(fused_kernel, out_shape=(jax.ShapeDtypeStruct((CAMS, 16, 5...  73.5 us
    unnamed x4, local copies, waits for them, and re-layouts  2.92 us

profile of v3, /device:TPU:1, one launch (start us, length us, event | category | flops | bytes accessed | tf_op | source)
XLA Modules:
  0.0 77.1 jit_solution(9803416577892534733)
XLA Ops:
  0.6 73.5 %fused.1 = (f32[32,16,512]{2,1,0:T(8,128)}, f32[32,32]{1,0:T(8,128)}) custom-call(bf16[16,16,4096]{2,1,0:T(8,128)(2,1)} %photo_ref.1, s32[16]{0:T(128)} %cid_ref.1, bf16[256,256]{1,0:T(8,128)(2,1)} %constant.18.clone.rest_0_, bf16[8,256,128]{2,1,0:T(8,128)(2,1)} %constant.19.clone.rest_1_, bf16[512,384]{1,0:T(8,128)(2,1)} %constant.20.clone.rest_2_, ...), custom_call_target="tpu_custom_call" | custom-call | tf_op jit(solution)/shard_map/fused/pallas_call | solution.py:487
  74.1 0.0 copy-start
  74.1 2.3 %copy.15 = f32[32,16,512]{2,1,0:T(8,128)} copy(f32[32,16,512]{2,1,0:T(8,128)} %get-tuple-element.4) | data formatting | bytes 2097152
  76.5 0.0 copy-done
  76.5 0.6 copy.16
Async XLA Ops:
  74.1 2.3 %copy-start = (f32[32,32]{1,0:T(8,128)S(1)}, f32[32,32]{1,0:T(8,128)}, u32[]{:S(2)}) copy-start(f32[32,32]{1,0:T(8,128)} %get-tuple-element.5) | copy-start | bytes 12292

commit v4 on v3

--- a/solution.py
+++ b/solution.py
@@ -22,6 +22,9 @@
 HR = 8
 LANES = 1024
 VMEM_LIMIT = 60 * 1024 * 1024
+
+MOVES = ((0, 0), (0, 1), (3, 0), (1, 0), (1, 1), (3, 1), (2, 0), (2, 1))
+ISSUE = (1, 3, 2, 6, 4, 5, 7)
 
 
 def constants():
@@ -36,13 +39,6 @@
             edge[jt, 120 + k, 16 * jt + k] = 1.0
             edge[jt, 128 + k, 16 * jt + 8 + k] = 1.0
     sign = np.array([[1, 1, 1], [1, -1, -1], [-1, 1, -1], [-1, -1, 1]], np.float32) * 0.5
-    haar = np.zeros((512, 384), np.float32)
-    for j in range(128):
-        for b in range(3):
-            haar[2 * j, 128 * b + j] = sign[0, b]
-            haar[2 * j + 1, 128 * b + j] = sign[1, b]
-            haar[256 + 2 * j, 128 * b + j] = sign[2, b]
-            haar[256 + 2 * j + 1, 128 * b + j] = sign[3, b]
     haar_edge = np.zeros((128, 512), np.float32)
     for j in range(4):
         for k in range(8):
@@ -52,8 +48,8 @@
                     haar_edge[at, 128 * j + 8 * b + k] = sign[n, b]
     split = np.zeros((256, 256), np.float32)
     for j in range(128):
-        split[2 * j, j] = 1.0
-        split[2 * j + 1, 128 + j] = 1.0
+        split[2 * j, j] = 0.5
+        split[2 * j + 1, 128 + j] = 0.5
     out = np.arange(256)
     box = np.zeros((4, 512, 256), np.float32)
     box_edge = np.zeros((4, 3, 256, 256), np.float32)
@@ -70,7 +66,7 @@
     fold = np.zeros((256, 128), np.float32)
     fold[np.arange(256), np.arange(256) // HR] = 1.0
     fold = np.concatenate([fold] * 3)
-    every = (perm, edge, haar, haar_edge, split, join, fold, box, box_edge)
+    every = (perm, edge, haar_edge, split, join, fold, box, box_edge)
     return [jnp.asarray(c, BF16) for c in every]
 
 
@@ -84,26 +80,33 @@
     return hi, lo
 
 
+def bands_of(px_ref, n):
+    a, b, c, d = (px_ref[j, n] for j in range(4))
+    plus, minus, low_plus, low_minus = a + b, a - b, c + d, c - d
+    return plus - low_plus, minus + low_minus, minus - low_minus
+
+
 def chunk(s, x_ref, e_ref, consts, scratch):
-    haar_ref, haar_edge_ref, split_ref, _, _, box_ref, box_edge_ref = consts[2:]
-    sq_ref, eq_ref, band_ref, lhs_ref, edge_ref, sum_ref, side_ref, px_ref, data_ref, acc_ref = scratch
+    haar_edge_ref, split_ref, _, _, box_ref, box_edge_ref = consts[2:]
+    sq_ref, eq_ref, lhs_ref, edge_ref, sum_ref, side_ref, px_ref, data_ref, acc_ref = scratch
 
     rows = 2 * HR
     for ct in range(2):
-        x = x_ref[s, :, :, 512 * ct : 512 * ct + 512].reshape(rows * OWN, 512)
-        got = dot(x, haar_ref[...])
-        for b in range(3):
-            one = got[:, 128 * b : 128 * b + 128].reshape(rows, OWN, 128)
-            band_ref[b, :, :, 128 * ct : 128 * ct + 128] = one[4 : 4 + HR]
-            sq_ref[b, :, :, 128 * ct : 128 * ct + 128] = one * one
         for tb in range(2):
             lane = 512 * ct + 256 * tb
-            x = x_ref[s, pl.ds(4, HR), :, lane : lane + 256].reshape(HR * OWN, 256)
+            x = x_ref[s, :, :, lane : lane + 256].reshape(rows * OWN, 256)
             got = dot(x, split_ref[...])
             for odd in range(2):
                 px_ref[2 * tb + odd, :, :, 128 * ct : 128 * ct + 128] = got[
                     :, 128 * odd : 128 * odd + 128
-                ].reshape(HR, OWN, 128)
+                ].reshape(rows, OWN, 128)
+
+    def squares(n, _):
+        for b, band in enumerate(bands_of(px_ref, n)):
+            sq_ref[b, n] = band * band
+        return 0
+
+    lax.fori_loop(0, rows, squares, 0, unroll=2)
     x = jnp.concatenate([e_ref[s, n] for n in (0, 1, 2, 4)])
     one = dot(x, haar_edge_ref[...])
     for n in range(rows):
@@ -138,19 +141,19 @@
 
     def residual(i, _):
         res = []
-        for b in range(3):
+        for b, band in enumerate(bands_of(px_ref, i + 4)):
             var = None
             for r in range(4):
                 mean = (sum_ref[r, b, i] + side_ref[r, b, i]) * (1.0 / (2 * r + 3) ** 2)
                 var = mean if var is None else jnp.minimum(var, mean)
             gain = NOISE_POWER / jnp.maximum(var, NOISE_POWER)
-            res.append(band_ref[b, i] * gain * 0.5)
+            res.append(band * gain * 0.5)
         hz, vt, dg = res
         plus, minus = hz + vt, hz - vt
         noise = (plus + dg, minus - dg, -minus - dg, dg - plus)
         at = pl.multiple_of(i * OWN, OWN)
         for j in range(4):
-            x = px_ref[j, i]
+            x = px_ref[j, i + 4]
             for part, value in enumerate((noise[j].astype(BF16).astype(F32) * x, x * x)):
                 hi, lo = hi_lo(value)
                 data_ref[2 * j + part, pl.ds(at, OWN), :] = hi
@@ -189,27 +192,31 @@
     col = lax.broadcasted_iota(jnp.int32, (256, 256), 1)
     gram = jnp.where(lax.rem(row, HR) == lax.rem(col, HR), gram, 0.0)
     gram = gram.reshape(CAMS, HR, 256).sum(axis=1)
-    gram = dot(three(gram), fold_ref[...])
+    gram = dot(three(gram), fold_ref[...]) * 0.25
     total = planes[0] + planes[1] + planes[2] + planes[3]
-    total = total.reshape(CAMS, HR, 256).sum(axis=1).sum(axis=1, keepdims=True)
+    total = total.reshape(CAMS, HR, 256).sum(axis=1).sum(axis=1, keepdims=True) * 0.5
+    row = lax.broadcasted_iota(jnp.int32, (CAMS, 128), 0)
+    lane = lax.broadcasted_iota(jnp.int32, (CAMS, 128), 1)
+    gram = jnp.where(lane == lax.rem(row + CAMS - 1, CAMS), total, gram)
     lane = lax.broadcasted_iota(jnp.int32, (8, 128), 1)
-    upper, lower = jnp.zeros((8, 128), F32), jnp.zeros((8, 128), F32)
-    for q in range(4):
-        part = gram[8 * q : 8 * q + 8]
-        if q:
-            part = pltpu.roll(part, 32 * q, 1)
-        upper = jnp.where(lane // 32 == q, part, upper)
-        lower = jnp.where(lane == q, total[8 * q : 8 * q + 8], lower)
-    return planes, jnp.concatenate([upper, lower])
+    sums = gram[0:8]
+    for q in range(1, 4):
+        part = pltpu.roll(gram[8 * q : 8 * q + 8], 32 * q, 1)
+        sums = jnp.where(lane // 32 == q, part, sums)
+    return planes, sums
 
 
 def correlated(sums):
-    upper, lower = sums[0:8], sums[8:16]
-    gram = jnp.concatenate([upper] + [pltpu.roll(upper, 128 - 32 * q, 1) for q in range(1, 4)])
-    total = jnp.concatenate([lower[:, q : q + 1] for q in range(4)])
-    pixels = float(256 * 4096)
+    gram = jnp.concatenate([sums] + [pltpu.roll(sums, 128 - 32 * q, 1) for q in range(1, 4)])
     row = lax.broadcasted_iota(jnp.int32, gram.shape, 0)
     lane = lax.broadcasted_iota(jnp.int32, gram.shape, 1)
+    before = lane == lax.rem(row + CAMS - 1, CAMS)
+    total = jnp.sum(jnp.where(before, gram, 0.0), axis=1, keepdims=True)
+    after = (row == lax.rem(lane + CAMS - 1, CAMS)) & (lane < CAMS)
+    along = jnp.sum(jnp.where(after, gram, 0.0), axis=0, keepdims=True)
+    down = jnp.sum(jnp.where(row == lane, along, 0.0), axis=1, keepdims=True)
+    gram = jnp.where(before, down, gram)
+    pixels = float(256 * 4096)
     average = total / pixels
     across = jnp.sum(jnp.where(row == lane, average, 0.0), axis=0, keepdims=True)
     covar = gram / pixels - average * across
@@ -263,14 +270,26 @@
         side_ref[d, 2] = ids
 
 
-N_CONST = 9
+N_CONST = 8
+
+
+def moved(me, k, sign):
+    if isinstance(k, int):
+        dy, dx = MOVES[k]
+    else:
+        dy, dx = 0, 0
+        for n in range(1, PH):
+            dy = jnp.where(k == n, MOVES[n][0], dy)
+            dx = jnp.where(k == n, MOVES[n][1], dx)
+    y, x = me // 2, lax.rem(me, 2)
+    return lax.rem(y + 4 + sign * dy, 4) * 2 + lax.rem(x + dx, 2)
 
 
 def fused_kernel(photo_ref, cid_ref, *rest):
     const_hbm, rest = rest[:N_CONST], rest[N_CONST:]
-    fp_ref, corr_ref, block_ref, side_ref, beside_ref, x_ref, e_ref, rows_ref, a_ref, b_ref = rest[:10]
+    fp_ref, sums_ref, block_ref, side_ref, beside_ref, x_ref, e_ref, rows_ref, a_ref, b_ref = rest[:10]
     consts, rest = rest[10 : 10 + N_CONST], rest[10 + N_CONST :]
-    scratch, rest = rest[:10], rest[10:]
+    scratch, rest = rest[:9], rest[9:]
     acc_ref = scratch[-1]
     (const_sem, own_sem, send_sem, recv_sem, up_send, up_recv, dn_send, dn_recv,
      as_sem, ar_sem, bs_sem, br_sem) = rest
@@ -293,6 +312,10 @@
             barrier, inc=1, device_id={"tile": lax.rem(t + k, TI)}, device_id_type=MESH
         )
 
+    for k in range(1, PH):
+        where = {"photo": lax.rem(me + k, PH), "tile": lax.rem(t + TI // 2, TI)}
+        pl.semaphore_signal(barrier, inc=1, device_id=where, device_id_type=MESH)
+
     @pl.when(middle == 1)
     def _():
         for k in range(1, PH):
@@ -302,7 +325,7 @@
     load(0).wait()
     load(1).wait()
     pack(photo_ref, cid_ref, consts[0], consts[1], block_ref, side_ref, beside_ref)
-    pl.semaphore_wait(barrier, PH + TI - 2 + (PH - 1) * middle)
+    pl.semaphore_wait(barrier, 2 * PH + TI - 3 + (PH - 1) * middle)
 
     def remote(srcs, dsts, send, recv, k, where):
         return [
@@ -314,7 +337,7 @@
         ]
 
     def a2a(k):
-        peer = lax.rem(me + k, PH)
+        peer = moved(me, k, 1)
         return remote(
             (block_ref.at[peer], side_ref.at[peer]),
             (x_ref.at[me, pl.ds(4, HR)], e_ref.at[me, pl.ds(1, 3)]),
@@ -339,20 +362,21 @@
         for copy in copies:
             getattr(copy, act)()
 
-    for k in range(1, PH):
+    def over_middle(k):
+        peer = moved(me, k, 1)
+
+        @pl.when(t == TI // 2 - 1)
+        def _():
+            each(down(k, mine(peer, False), me, {"photo": peer, "tile": t + 1}), "start")
+
+        @pl.when(t == TI // 2)
+        def _():
+            each(up(k, mine(peer, True), me, {"photo": peer, "tile": t - 1}), "start")
+
+    for k in ISSUE:
         each(a2a(k), "start")
-
-    @pl.when(t == TI // 2 - 1)
-    def _():
-        for k in range(PH):
-            peer = lax.rem(me + k, PH)
-            each(down(k, mine(peer, False), me, {"photo": peer, "tile": t + 1}), "start")
-
-    @pl.when(t == TI // 2)
-    def _():
-        for k in range(PH):
-            peer = lax.rem(me + k, PH)
-            each(up(k, mine(peer, True), me, {"photo": peer, "tile": t - 1}), "start")
+    for k in range(PH):
+        over_middle(k)
 
     def pass_on(k, source, s):
         @pl.when((t > 0) & (t != TI // 2))
@@ -386,11 +410,11 @@
         load(n).wait()
 
     def step(k, _):
-        s = lax.rem(me + PH - k, PH)
+        s = moved(me, k, -1)
 
         @pl.when(k < PH - 1)
         def _():
-            after = lax.rem(me + PH - 1 - k, PH)
+            after = moved(me, k + 1, -1)
             each(a2a(k + 1), "wait_recv")
             pass_on(k + 1, held, after)
 
@@ -407,25 +431,31 @@
 
     lax.fori_loop(0, PH, step, 0)
 
+    place = lax.rem(t, 8)
+    plane = me * 2 + t // 8
+
     def first(k):
+        to = lax.rem(plane + k, 16)
         return pltpu.make_async_remote_copy(
-            src_ref=a_ref.at[me], dst_ref=a_ref.at[me], send_sem=as_sem.at[k],
+            src_ref=a_ref.at[plane], dst_ref=a_ref.at[plane], send_sem=as_sem.at[k],
             recv_sem=ar_sem.at[k],
-            device_id={"photo": lax.rem(me + k, PH)}, device_id_type=MESH,
+            device_id={"photo": to // 2, "tile": lax.rem(to, 2) * 8 + place},
+            device_id_type=MESH,
         )
 
     def second(k):
+        to = lax.rem(place + k, 8)
         return pltpu.make_async_remote_copy(
-            src_ref=b_ref.at[t], dst_ref=b_ref.at[t], send_sem=bs_sem.at[k],
+            src_ref=b_ref.at[place], dst_ref=b_ref.at[place], send_sem=bs_sem.at[k],
             recv_sem=br_sem.at[k],
-            device_id={"tile": lax.rem(t + k, TI)}, device_id_type=MESH,
+            device_id={"tile": t // 8 * 8 + to}, device_id_type=MESH,
         )
 
-    planes, sums = total_gram(acc_ref, consts[6])
-    a_ref[me] = sums
-    for k in range(1, PH):
+    planes, sums = total_gram(acc_ref, consts[5])
+    a_ref[plane] = sums
+    for k in range(1, 16):
         first(k).start()
-    join(planes, consts[5], rows_ref)
+    join(planes, consts[4], rows_ref)
     out = [
         pltpu.make_async_copy(
             rows_ref.at[n], fp_ref.at[:, :, pl.ds(128 * n, 128)], own_sem.at[2 + n]
@@ -433,29 +463,29 @@
         for n in range(4)
     ]
     each(out, "start")
-    for k in range(1, PH):
+    for k in range(1, 16):
         first(k).wait_recv()
     sums = a_ref[0]
-    for n in range(1, PH):
+    for n in range(1, 16):
         sums += a_ref[n]
-    b_ref[t] = sums
-    for k in range(1, TI):
+    b_ref[place] = sums
+    for k in range(1, 8):
         second(k).start()
-    for k in range(1, TI):
+    for k in range(1, 8):
         second(k).wait_recv()
     sums = b_ref[0]
-    for n in range(1, TI):
+    for n in range(1, 8):
         sums += b_ref[n]
-    corr_ref[...] = correlated(sums)
+    sums_ref[...] = sums
 
     each(out, "wait")
     for k in range(1, PH):
         each(a2a(k), "wait_send")
+        second(k).wait_send()
+    for k in range(1, 16):
         first(k).wait_send()
-    for k in range(1, TI):
-        second(k).wait_send()
     for k in range(PH):
-        s = lax.rem(me + PH - k, PH)
+        s = moved(me, k, -1)
 
         @pl.when(t > 0)
         def _():
@@ -469,12 +499,11 @@
 SCRATCH = [
     ((3, 2 * HR, OWN, 256), F32),
     ((2 * HR, OWN, 128), F32),
-    ((3, HR, OWN, 256), F32),
     ((4, 3, HR, OWN, 512), BF16),
     ((4, HR, OWN, 256), BF16),
     ((4, 3, HR, OWN, 256), F32),
     ((4, 3, HR, OWN, 256), F32),
-    ((4, HR, OWN, 256), F32),
+    ((4, 2 * HR, OWN, 256), F32),
     ((8, 256, 256), BF16),
     ((8, 256, 256), F32),
 ]
@@ -488,7 +517,7 @@
         fused_kernel,
         out_shape=(
             jax.ShapeDtypeStruct((CAMS, 16, 512), F32),
-            jax.ShapeDtypeStruct((CAMS, CAMS), F32),
+            jax.ShapeDtypeStruct((8, 128), F32),
         ),
         in_specs=[vm, pl.BlockSpec(memory_space=pltpu.SMEM)] + [anywhere] * N_CONST,
         out_specs=(anywhere, vm),
@@ -499,15 +528,15 @@
             pltpu.VMEM((PH, 2 * HR, OWN, LANES), BF16),
             pltpu.VMEM((PH, 5, OWN, 128), BF16),
             pltpu.VMEM((4, CAMS, 16, 128), F32),
-            pltpu.VMEM((PH, 16, 128), F32),
-            pltpu.VMEM((TI, 16, 128), F32),
+            pltpu.VMEM((16, 8, 128), F32),
+            pltpu.VMEM((8, 8, 128), F32),
         ]
         + [pltpu.VMEM(c.shape, c.dtype) for c in consts]
         + [pltpu.VMEM(s, d) for s, d in SCRATCH]
         + [dma((N_CONST,)), dma((6,))]
         + [dma((2, PH))] * 6
-        + [dma((PH,))] * 2
-        + [dma((TI,))] * 2,
+        + [dma((16,))] * 2
+        + [dma((8,))] * 2,
         compiler_params=pltpu.CompilerParams(
             collective_id=0, has_side_effects=True, vmem_limit_bytes=VMEM_LIMIT
         ),
@@ -515,8 +544,31 @@
     )(photos, camera_id, *consts)
 
 
+def last_kernel(raw_ref, sums_ref, fp_ref, corr_ref):
+    fp_ref[...] = raw_ref[...]
+
+    @pl.when(pl.program_id(0) == 0)
+    def _():
+        corr_ref[...] = correlated(sums_ref[...])
+
+
+def last(raw, sums):
+    part = pl.BlockSpec((8, 16, 512), lambda n: (n, 0, 0))
+    return pl.pallas_call(
+        last_kernel,
+        grid=(CAMS // 8,),
+        out_shape=(
+            jax.ShapeDtypeStruct((CAMS, 16, 512), F32),
+            jax.ShapeDtypeStruct((CAMS, CAMS), F32),
+        ),
+        in_specs=[part, pl.BlockSpec((8, 128), lambda n: (0, 0))],
+        out_specs=(part, pl.BlockSpec((CAMS, CAMS), lambda n: (0, 0))),
+        name="last",
+    )(raw, sums)
+
+
 def on_device(photos, camera_id):
-    return fused(photos, camera_id, constants())
+    return last(*fused(photos, camera_id, constants()))
 
 
 def solution(mesh):

time: 77.2 us -> 75.9 us (0.983)
  local copies, waits for them, and re-layouts: 2.92 us -> 0 us
  Pallas kernels: 73.5 us -> 75.1 us
    pallas_call x0 -> x1, Pallas kernels: none -> 3.63 us  [last(): pl.pallas_call(last_kernel, grid=(CAMS // 8,), out_shape=(jax.ShapeDtypeS...]
    unnamed x4 -> x0, local copies, waits for them, and re-layouts: 2.92 us -> none
    pallas_call x1, Pallas kernels: 73.5 us -> 71.4 us  [fused(): pl.pallas_call(fused_kernel, out_shape=(jax.ShapeDtypeStruct((CAMS, 16, 5...]
where the time goes in v4:
time: 75.9 us; the launch traced here: 75.7 us
  Pallas kernels  75.1 us (99%)
    pallas_call x1, Pallas kernels, fused(): pl.pallas_call(fused_kernel, out_shape=(jax.ShapeDtypeStruct((CAMS, 16, 5...  71.4 us
    pallas_call x1, Pallas kernels, last(): pl.pallas_call(last_kernel, grid=(CAMS // 8,), out_shape=(jax.ShapeDtypeS...  3.63 us

profile of v4, /device:TPU:1, one launch (start us, length us, event | category | flops | bytes accessed | tf_op | source)
XLA Modules:
  0.0 75.7 jit_solution(14987065931294700711)
XLA Ops:
  0.6 71.4 %fused.1 = (f32[32,16,512]{2,1,0:T(8,128)}, f32[8,128]{1,0:T(8,128)}) custom-call(bf16[16,16,4096]{2,1,0:T(8,128)(2,1)} %photo_ref.1, s32[16]{0:T(128)} %cid_ref.1, bf16[256,256]{1,0:T(8,128)(2,1)} %constant.16.clone.rest_0_, bf16[8,256,128]{2,1,0:T(8,128)(2,1)} %constant.17.clone.rest_1_, bf16[128,512]{1,0:T(8,128)(2,1)} %constant.18.clone.rest_2_, ...), custom_call_target="tpu_custom_call" | custom-call | tf_op jit(solution)/shard_map/fused/pallas_call | solution.py:516
  72.1 3.6 %last.1 = (f32[32,16,512]{2,1,0:T(8,128)}, f32[32,32]{1,0:T(8,128)}) custom-call(f32[32,16,512]{2,1,0:T(8,128)} %get-tuple-element.4.raw_ref, f32[8,128]{1,0:T(8,128)} %get-tuple-element.5.sums_ref), custom_call_target="tpu_custom_call" | custom-call | tf_op jit(solution)/shard_map/last/pallas_call | solution.py:557

commit v5 on v4

--- a/solution.py
+++ b/solution.py
@@ -24,7 +24,8 @@
 VMEM_LIMIT = 60 * 1024 * 1024
 
 MOVES = ((0, 0), (0, 1), (3, 0), (1, 0), (1, 1), (3, 1), (2, 0), (2, 1))
-ISSUE = (1, 3, 2, 6, 4, 5, 7)
+WAVES = ((1, 3, 2), (4, 6), (5,), (7,))
+ROUTES = ((0, 1), (2, 4), (3, 5), (6, 7))
 
 
 def constants():
@@ -287,12 +288,12 @@
 
 def fused_kernel(photo_ref, cid_ref, *rest):
     const_hbm, rest = rest[:N_CONST], rest[N_CONST:]
-    fp_ref, sums_ref, block_ref, side_ref, beside_ref, x_ref, e_ref, rows_ref, a_ref, b_ref = rest[:10]
-    consts, rest = rest[10 : 10 + N_CONST], rest[10 + N_CONST :]
+    fp_ref, sums_ref, block_ref, side_ref, beside_ref, x_ref, e_ref, rows_ref, a_ref, b_ref, by_ref, by_side_ref = rest[:12]
+    consts, rest = rest[12 : 12 + N_CONST], rest[12 + N_CONST :]
     scratch, rest = rest[:9], rest[9:]
     acc_ref = scratch[-1]
     (const_sem, own_sem, send_sem, recv_sem, up_send, up_recv, dn_send, dn_recv,
-     as_sem, ar_sem, bs_sem, br_sem) = rest
+     by_send, by_recv, as_sem, ar_sem, bs_sem, br_sem) = rest
     me = lax.axis_index("photo")
     t = lax.axis_index("tile")
 
@@ -304,6 +305,9 @@
 
     barrier = pltpu.get_barrier_semaphore()
     middle = t * (TI - 1 - t) // 56
+    half = t // (TI // 2)
+    inward = t + half * (TI - 1 - 2 * t)
+    relay = (1 - lax.rem(inward, 2)) * (1 - inward // 6)
     for k in range(1, PH):
         peer = lax.rem(me + k, PH)
         pl.semaphore_signal(barrier, inc=1, device_id={"photo": peer}, device_id_type=MESH)
@@ -321,16 +325,25 @@
         for k in range(1, PH):
             where = {"photo": lax.rem(me + k, PH), "tile": TI - 1 - t}
             pl.semaphore_signal(barrier, inc=1, device_id=where, device_id_type=MESH)
+            for q in range(1, 4):
+                where = {"photo": lax.rem(me + k, PH), "tile": (1 - half) * (9 + 2 * q) + half * (6 - 2 * q)}
+                pl.semaphore_signal(barrier, inc=1, device_id=where, device_id_type=MESH)
+
+    @pl.when(relay == 1)
+    def _():
+        for k in range(1, PH):
+            where = {"photo": lax.rem(me + k, PH), "tile": TI // 2 - half}
+            pl.semaphore_signal(barrier, inc=1, device_id=where, device_id_type=MESH)
 
     load(0).wait()
     load(1).wait()
     pack(photo_ref, cid_ref, consts[0], consts[1], block_ref, side_ref, beside_ref)
-    pl.semaphore_wait(barrier, 2 * PH + TI - 3 + (PH - 1) * middle)
-
-    def remote(srcs, dsts, send, recv, k, where):
+    pl.semaphore_wait(barrier, 2 * PH + TI - 3 + (PH - 1) * (4 * middle + relay))
+
+    def remote(srcs, dsts, send, k, recv, j, where):
         return [
             pltpu.make_async_remote_copy(
-                src_ref=a, dst_ref=b, send_sem=send.at[n, k], recv_sem=recv.at[n, k],
+                src_ref=a, dst_ref=b, send_sem=send.at[n, k], recv_sem=recv.at[n, j],
                 device_id=where, device_id_type=MESH,
             )
             for n, (a, b) in enumerate(zip(srcs, dsts))
@@ -341,16 +354,16 @@
         return remote(
             (block_ref.at[peer], side_ref.at[peer]),
             (x_ref.at[me, pl.ds(4, HR)], e_ref.at[me, pl.ds(1, 3)]),
-            send_sem, recv_sem, k, {"photo": peer},
+            send_sem, k, recv_sem, k, {"photo": peer},
         )
 
     def up(k, srcs, s, where):
         dsts = (x_ref.at[s, pl.ds(12, 4)], e_ref.at[s, 4])
-        return remote(srcs, dsts, up_send, up_recv, k, where)
+        return remote(srcs, dsts, up_send, k, up_recv, k, where)
 
     def down(k, srcs, s, where):
         dsts = (x_ref.at[s, pl.ds(0, 4)], e_ref.at[s, 0])
-        return remote(srcs, dsts, dn_send, dn_recv, k, where)
+        return remote(srcs, dsts, dn_send, k, dn_recv, k, where)
 
     def held(s, first):
         return (x_ref.at[s, pl.ds(4 if first else 8, 4)], e_ref.at[s, 1 if first else 2])
@@ -362,21 +375,58 @@
         for copy in copies:
             getattr(copy, act)()
 
-    def over_middle(k):
-        peer = moved(me, k, 1)
-
-        @pl.when(t == TI // 2 - 1)
-        def _():
-            each(down(k, mine(peer, False), me, {"photo": peer, "tile": t + 1}), "start")
-
-        @pl.when(t == TI // 2)
-        def _():
-            each(up(k, mine(peer, True), me, {"photo": peer, "tile": t - 1}), "start")
-
-    for k in ISSUE:
+    def over_middle(first):
+        act = up if first else down
+        for q in range(4):
+            for j, k in enumerate(ROUTES[q]):
+                peer = moved(me, k, 1)
+                if q == 0:
+                    where = {"photo": peer, "tile": TI // 2 - 1 if first else TI // 2}
+                    copies = act(k, mine(peer, first), me, where)
+                else:
+                    copies = remote(
+                        mine(peer, first), (by_ref.at[j], by_side_ref.at[j]),
+                        up_send if first else dn_send, k, by_recv, j,
+                        {"tile": 9 + 2 * q if first else 6 - 2 * q},
+                    )
+                each(copies, "start")
+
+    def relayed(q, j, first):
+        k = ROUTES[q][j]
+        if first:
+            dsts, recv = (x_ref.at[me, pl.ds(12, 4)], e_ref.at[me, 4]), up_recv
+        else:
+            dsts, recv = (x_ref.at[me, pl.ds(0, 4)], e_ref.at[me, 0]), dn_recv
+        where = {"photo": moved(me, k, 1), "tile": TI // 2 - 1 if first else TI // 2}
+        return remote((by_ref.at[j], by_side_ref.at[j]), dsts, by_send, j, recv, k, where)
+
+    def relays(act):
+        for q in range(1, 4):
+            for first in (False, True):
+
+                @pl.when(t == (9 + 2 * q if first else 6 - 2 * q))
+                def _():
+                    for j in range(2):
+                        act(q, j, first)
+
+    def forward(q, j, first):
+        landed = remote(
+            mine(me, first), (by_ref.at[j], by_side_ref.at[j]), by_send, j, by_recv, j,
+            {"tile": TI // 2 if first else TI // 2 - 1},
+        )
+        each(landed, "wait_recv")
+        each(relayed(q, j, first), "start")
+
+    @pl.when(t == TI // 2 - 1)
+    def _():
+        over_middle(False)
+
+    @pl.when(t == TI // 2)
+    def _():
+        over_middle(True)
+
+    for k in WAVES[0]:
         each(a2a(k), "start")
-    for k in range(PH):
-        over_middle(k)
 
     def pass_on(k, source, s):
         @pl.when((t > 0) & (t != TI // 2))
@@ -412,11 +462,13 @@
     def step(k, _):
         s = moved(me, k, -1)
 
-        @pl.when(k < PH - 1)
-        def _():
-            after = moved(me, k + 1, -1)
+        def ahead():
             each(a2a(k + 1), "wait_recv")
-            pass_on(k + 1, held, after)
+            pass_on(k + 1, held, moved(me, k + 1, -1))
+
+        @pl.when((k > 0) & (k < PH - 1))
+        def _():
+            ahead()
 
         @pl.when(t > 0)
         def _():
@@ -427,6 +479,22 @@
             each(up(k, held(s, True), s, {"tile": t + 1}), "wait_recv")
 
         chunk(s, x_ref, e_ref, consts, scratch)
+
+        @pl.when(k == 0)
+        def _():
+            relays(forward)
+
+        for n in range(1, 4):
+
+            @pl.when(k == n - 1)
+            def _():
+                for j in WAVES[n]:
+                    each(a2a(j), "start")
+
+        @pl.when(k == 0)
+        def _():
+            ahead()
+
         return 0
 
     lax.fori_loop(0, PH, step, 0)
@@ -479,6 +547,7 @@
     sums_ref[...] = sums
 
     each(out, "wait")
+    relays(lambda q, j, first: each(relayed(q, j, first), "wait_send"))
     for k in range(1, PH):
         each(a2a(k), "wait_send")
         second(k).wait_send()
@@ -530,11 +599,14 @@
             pltpu.VMEM((4, CAMS, 16, 128), F32),
             pltpu.VMEM((16, 8, 128), F32),
             pltpu.VMEM((8, 8, 128), F32),
+            pltpu.VMEM((2, 4, OWN, LANES), BF16),
+            pltpu.VMEM((2, OWN, 128), BF16),
         ]
         + [pltpu.VMEM(c.shape, c.dtype) for c in consts]
         + [pltpu.VMEM(s, d) for s, d in SCRATCH]
         + [dma((N_CONST,)), dma((6,))]
         + [dma((2, PH))] * 6
+        + [dma((2, 2))] * 2
         + [dma((16,))] * 2
         + [dma((8,))] * 2,
         compiler_params=pltpu.CompilerParams(
@@ -544,25 +616,43 @@
     )(photos, camera_id, *consts)
 
 
-def last_kernel(raw_ref, sums_ref, fp_ref, corr_ref):
-    fp_ref[...] = raw_ref[...]
-
-    @pl.when(pl.program_id(0) == 0)
-    def _():
-        corr_ref[...] = correlated(sums_ref[...])
+def last_kernel(raw_ref, sums_ref, fp_ref, corr_ref, held_ref, in_sem, out_sem):
+    parts = 4
+    rows = CAMS // parts
+    into = [
+        pltpu.make_async_copy(raw_ref.at[pl.ds(rows * n, rows)], held_ref.at[n], in_sem.at[n])
+        for n in range(parts)
+    ]
+    back = [
+        pltpu.make_async_copy(held_ref.at[n], fp_ref.at[pl.ds(rows * n, rows)], out_sem.at[n])
+        for n in range(parts)
+    ]
+    for copy in into:
+        copy.start()
+    corr_ref[...] = correlated(sums_ref[...])
+    for n in range(parts):
+        into[n].wait()
+        back[n].start()
+    for copy in back:
+        copy.wait()
 
 
 def last(raw, sums):
-    part = pl.BlockSpec((8, 16, 512), lambda n: (n, 0, 0))
+    vm = pl.BlockSpec(memory_space=pltpu.VMEM)
+    anywhere = pl.BlockSpec(memory_space=pl.ANY)
     return pl.pallas_call(
         last_kernel,
-        grid=(CAMS // 8,),
         out_shape=(
             jax.ShapeDtypeStruct((CAMS, 16, 512), F32),
             jax.ShapeDtypeStruct((CAMS, CAMS), F32),
         ),
-        in_specs=[part, pl.BlockSpec((8, 128), lambda n: (0, 0))],
-        out_specs=(part, pl.BlockSpec((CAMS, CAMS), lambda n: (0, 0))),
+        in_specs=[anywhere, vm],
+        out_specs=(anywhere, vm),
+        scratch_shapes=[
+            pltpu.VMEM((4, CAMS // 4, 16, 512), F32),
+            pltpu.SemaphoreType.DMA((4,)),
+            pltpu.SemaphoreType.DMA((4,)),
+        ],
         name="last",
     )(raw, sums)
 

time: 75.9 us -> 65.6 us (0.86)
  Pallas kernels: 75.1 us -> 64.8 us
    pallas_call x1, Pallas kernels: 71.4 us -> 61.5 us  [fused(): pl.pallas_call(fused_kernel, out_shape=(jax.ShapeDtypeStruct((CAMS, 16, 5...]
where the time goes in v5:
time: 65.6 us; the launch traced here: 65.4 us
  Pallas kernels  64.8 us (99%)
    pallas_call x1, Pallas kernels, fused(): pl.pallas_call(fused_kernel, out_shape=(jax.ShapeDtypeStruct((CAMS, 16, 5...  61.5 us
    pallas_call x1, Pallas kernels, last(): pl.pallas_call(last_kernel, out_shape=(jax.ShapeDtypeStruct((CAMS, 16, 51...  3.26 us

profile of v5, /device:TPU:1, one launch (start us, length us, event | category | flops | bytes accessed | tf_op | source)
XLA Modules:
  0.0 65.4 jit_solution(13027588541767127481)
XLA Ops:
  0.6 61.5 %fused.1 = (f32[32,16,512]{2,1,0:T(8,128)}, f32[8,128]{1,0:T(8,128)}) custom-call(bf16[16,16,4096]{2,1,0:T(8,128)(2,1)} %photo_ref.1, s32[16]{0:T(128)} %cid_ref.1, bf16[256,256]{1,0:T(8,128)(2,1)} %constant.16.clone.rest_0_, bf16[8,256,128]{2,1,0:T(8,128)(2,1)} %constant.17.clone.rest_1_, bf16[128,512]{1,0:T(8,128)(2,1)} %constant.18.clone.rest_2_, ...), custom_call_target="tpu_custom_call" | custom-call | tf_op jit(solution)/shard_map/fused/pallas_call | solution.py:585
  62.2 3.3 %last.1 = (f32[32,16,512]{2,1,0:T(8,128)}, f32[32,32]{1,0:T(8,128)}) custom-call(f32[32,16,512]{2,1,0:T(8,128)} %get-tuple-element.4.raw_ref, f32[8,128]{1,0:T(8,128)} %get-tuple-element.5.sums_ref), custom_call_target="tpu_custom_call" | custom-call | tf_op jit(solution)/shard_map/last/pallas_call | solution.py:643

commit v6 on v5

--- a/solution.py
+++ b/solution.py
@@ -52,17 +52,17 @@
         split[2 * j, j] = 0.5
         split[2 * j + 1, 128 + j] = 0.5
     out = np.arange(256)
-    box = np.zeros((4, 512, 256), np.float32)
-    box_edge = np.zeros((4, 3, 256, 256), np.float32)
+    box = np.zeros((4, 256, 256), np.float32)
+    box_edge = np.zeros((4, 3, 128, 256), np.float32)
     for r in range(1, 5):
         inner = (np.abs(out[:, None] - out[None, :]) <= r).astype(np.float32)
-        box[r - 1] = np.concatenate([inner, inner])
+        box[r - 1] = inner
         for b in range(3):
             side = np.zeros((128, 256), np.float32)
             for k in range(8):
                 cell = k - 4 if k < 4 else 252 + k
                 side[8 * b + k] = np.abs(cell - out) <= r
-            box_edge[r - 1, b] = np.concatenate([side, side])
+            box_edge[r - 1, b] = side
     join = np.concatenate([split.T] * 3)
     fold = np.zeros((256, 128), np.float32)
     fold[np.arange(256), np.arange(256) // HR] = 1.0
@@ -237,11 +237,12 @@
                 rows_ref[2 * ct + part, :, pl.ds(tb, HR, stride=2), :] = one
 
 
-def pack(photo_ref, cid_ref, perm_ref, edge_ref, block_ref, side_ref, beside_ref):
+def pack(fetch, photo_ref, cid_ref, perm_ref, edge_ref, block_ref, side_ref, beside_ref):
     beside_ref[:, 1, :, :, 0:128] = jnp.zeros((8, 2, OWN, 128), BF16)
     beside_ref[:, PH, :, :, 128:256] = jnp.zeros((8, 2, OWN, 128), BF16)
 
     def block(d, _):
+        fetch(d).wait()
         for ct in range(2):
             lane = pl.multiple_of(512 * d + 256 * ct, 256)
             x = photo_ref[:, :, pl.ds(lane, 256)].reshape(256, 256)
@@ -286,22 +287,43 @@
     return lax.rem(y + 4 + sign * dy, 4) * 2 + lax.rem(x + dx, 2)
 
 
-def fused_kernel(photo_ref, cid_ref, *rest):
+def fused_kernel(photo_hbm, cid_ref, *rest):
     const_hbm, rest = rest[:N_CONST], rest[N_CONST:]
-    fp_ref, sums_ref, block_ref, side_ref, beside_ref, x_ref, e_ref, rows_ref, a_ref, b_ref, by_ref, by_side_ref = rest[:12]
-    consts, rest = rest[12 : 12 + N_CONST], rest[12 + N_CONST :]
+    fp_ref, sums_ref, block_ref, side_ref, beside_ref, x_ref, e_ref, rows_ref, a_ref, b_ref, by_ref, by_side_ref, photo_ref = rest[:13]
+    consts, rest = rest[13 : 13 + N_CONST], rest[13 + N_CONST :]
     scratch, rest = rest[:9], rest[9:]
     acc_ref = scratch[-1]
-    (const_sem, own_sem, send_sem, recv_sem, up_send, up_recv, dn_send, dn_recv,
+    (photo_sem, const_sem, own_sem, send_sem, recv_sem, up_send, up_recv, dn_send, dn_recv,
      by_send, by_recv, as_sem, ar_sem, bs_sem, br_sem) = rest
     me = lax.axis_index("photo")
     t = lax.axis_index("tile")
 
     def load(n):
-        return pltpu.make_async_copy(const_hbm[n], consts[n], const_sem.at[n])
-
+        if n < N_CONST - 2:
+            return [pltpu.make_async_copy(const_hbm[n], consts[n], const_sem.at[n, 0])]
+        depth = consts[n].shape[-2] // 2
+        lead = (slice(None),) * (len(consts[n].shape) - 2)
+        return [
+            pltpu.make_async_copy(
+                const_hbm[n], consts[n].at[(*lead, pl.ds(depth * part, depth))], const_sem.at[n, part]
+            )
+            for part in range(2)
+        ]
+
+    def fetch(d):
+        lanes = pl.ds(pl.multiple_of(512 * d, 512), 512)
+        return pltpu.make_async_copy(
+            photo_hbm.at[:, :, lanes], photo_ref.at[:, :, lanes], photo_sem.at[d]
+        )
+
+    def each(copies, act):
+        for copy in copies:
+            getattr(copy, act)()
+
+    for d in range(PH):
+        fetch(d).start()
     for n in range(N_CONST):
-        load(n).start()
+        each(load(n), "start")
 
     barrier = pltpu.get_barrier_semaphore()
     middle = t * (TI - 1 - t) // 56
@@ -335,9 +357,9 @@
             where = {"photo": lax.rem(me + k, PH), "tile": TI // 2 - half}
             pl.semaphore_signal(barrier, inc=1, device_id=where, device_id_type=MESH)
 
-    load(0).wait()
-    load(1).wait()
-    pack(photo_ref, cid_ref, consts[0], consts[1], block_ref, side_ref, beside_ref)
+    each(load(0), "wait")
+    each(load(1), "wait")
+    pack(fetch, photo_ref, cid_ref, consts[0], consts[1], block_ref, side_ref, beside_ref)
     pl.semaphore_wait(barrier, 2 * PH + TI - 3 + (PH - 1) * (4 * middle + relay))
 
     def remote(srcs, dsts, send, k, recv, j, where):
@@ -370,10 +392,6 @@
 
     def mine(d, first):
         return (block_ref.at[d, pl.ds(0 if first else 4, 4)], side_ref.at[d, 0 if first else 1])
-
-    def each(copies, act):
-        for copy in copies:
-            getattr(copy, act)()
 
     def over_middle(first):
         act = up if first else down
@@ -457,7 +475,7 @@
     acc_ref[...] = jnp.zeros(acc_ref.shape, F32)
     each(own, "wait")
     for n in range(2, N_CONST):
-        load(n).wait()
+        each(load(n), "wait")
 
     def step(k, _):
         s = moved(me, k, -1)
@@ -588,7 +606,7 @@
             jax.ShapeDtypeStruct((CAMS, 16, 512), F32),
             jax.ShapeDtypeStruct((8, 128), F32),
         ),
-        in_specs=[vm, pl.BlockSpec(memory_space=pltpu.SMEM)] + [anywhere] * N_CONST,
+        in_specs=[anywhere, pl.BlockSpec(memory_space=pltpu.SMEM)] + [anywhere] * N_CONST,
         out_specs=(anywhere, vm),
         scratch_shapes=[
             pltpu.VMEM((PH, HR, OWN, LANES), BF16),
@@ -601,10 +619,12 @@
             pltpu.VMEM((8, 8, 128), F32),
             pltpu.VMEM((2, 4, OWN, LANES), BF16),
             pltpu.VMEM((2, OWN, 128), BF16),
+            pltpu.VMEM((OWN, 16, 4096), BF16),
         ]
-        + [pltpu.VMEM(c.shape, c.dtype) for c in consts]
+        + [pltpu.VMEM(c.shape, c.dtype) for c in consts[:-2]]
+        + [pltpu.VMEM((*c.shape[:-2], 2 * c.shape[-2], 256), c.dtype) for c in consts[-2:]]
         + [pltpu.VMEM(s, d) for s, d in SCRATCH]
-        + [dma((N_CONST,)), dma((6,))]
+        + [dma((PH,)), dma((N_CONST, 2)), dma((6,))]
         + [dma((2, PH))] * 6
         + [dma((2, 2))] * 2
         + [dma((16,))] * 2
@@ -616,29 +636,30 @@
     )(photos, camera_id, *consts)
 
 
-def last_kernel(raw_ref, sums_ref, fp_ref, corr_ref, held_ref, in_sem, out_sem):
+def last_kernel(raw_ref, sums_hbm, fp_ref, corr_hbm, held_ref, sums_ref, corr_ref, in_sem, out_sem):
     parts = 4
     rows = CAMS // parts
-    into = [
+    into = [pltpu.make_async_copy(sums_hbm, sums_ref, in_sem.at[parts])] + [
         pltpu.make_async_copy(raw_ref.at[pl.ds(rows * n, rows)], held_ref.at[n], in_sem.at[n])
         for n in range(parts)
     ]
-    back = [
+    back = [pltpu.make_async_copy(corr_ref, corr_hbm, out_sem.at[parts])] + [
         pltpu.make_async_copy(held_ref.at[n], fp_ref.at[pl.ds(rows * n, rows)], out_sem.at[n])
         for n in range(parts)
     ]
     for copy in into:
         copy.start()
-    corr_ref[...] = correlated(sums_ref[...])
-    for n in range(parts):
+    for n in range(1, parts + 1):
         into[n].wait()
         back[n].start()
+    into[0].wait()
+    corr_ref[...] = correlated(sums_ref[...])
+    back[0].start()
     for copy in back:
         copy.wait()
 
 
 def last(raw, sums):
-    vm = pl.BlockSpec(memory_space=pltpu.VMEM)
     anywhere = pl.BlockSpec(memory_space=pl.ANY)
     return pl.pallas_call(
         last_kernel,
@@ -646,12 +667,14 @@
             jax.ShapeDtypeStruct((CAMS, 16, 512), F32),
             jax.ShapeDtypeStruct((CAMS, CAMS), F32),
         ),
-        in_specs=[anywhere, vm],
-        out_specs=(anywhere, vm),
+        in_specs=[anywhere, anywhere],
+        out_specs=(anywhere, anywhere),
         scratch_shapes=[
             pltpu.VMEM((4, CAMS // 4, 16, 512), F32),
-            pltpu.SemaphoreType.DMA((4,)),
-            pltpu.SemaphoreType.DMA((4,)),
+            pltpu.VMEM((8, 128), F32),
+            pltpu.VMEM((CAMS, CAMS), F32),
+            pltpu.SemaphoreType.DMA((5,)),
+            pltpu.SemaphoreType.DMA((5,)),
         ],
         name="last",
     )(raw, sums)

time: 65.6 us -> 63.7 us (0.971)
  Pallas kernels: 64.8 us -> 62.9 us
    pallas_call x1, Pallas kernels: 3.26 us -> 2.14 us  [last(): pl.pallas_call(last_kernel, out_shape=(jax.ShapeDtypeStruct((CAMS, 16, 51...]
    pallas_call x1, Pallas kernels: 61.5 us -> 60.8 us  [fused(): pl.pallas_call(fused_kernel, out_shape=(jax.ShapeDtypeStruct((CAMS, 16, 5...]
where the time goes in v6:
time: 63.7 us; the launch traced here: 63.5 us
  Pallas kernels  62.9 us (99%)
  between operations  0.64 us (1%)
    pallas_call x1, Pallas kernels, fused(): pl.pallas_call(fused_kernel, out_shape=(jax.ShapeDtypeStruct((CAMS, 16, 5...  60.8 us
    pallas_call x1, Pallas kernels, last(): pl.pallas_call(last_kernel, out_shape=(jax.ShapeDtypeStruct((CAMS, 16, 51...  2.14 us

profile of v6, /device:TPU:1, one launch (start us, length us, event | category | flops | bytes accessed | tf_op | source)
XLA Modules:
  0.0 63.5 jit_solution(2681221295435284245)
XLA Ops:
  0.6 60.8 %fused.1 = (f32[32,16,512]{2,1,0:T(8,128)}, f32[8,128]{1,0:T(8,128)}) custom-call(bf16[16,16,4096]{2,1,0:T(8,128)(2,1)} %photo_hbm.1, s32[16]{0:T(128)} %cid_ref.1, bf16[256,256]{1,0:T(8,128)(2,1)} %constant.16.clone.rest_0_, bf16[8,256,128]{2,1,0:T(8,128)(2,1)} %constant.17.clone.rest_1_, bf16[128,512]{1,0:T(8,128)(2,1)} %constant.18.clone.rest_2_, ...), custom_call_target="tpu_custom_call" | custom-call | tf_op jit(solution)/shard_map/fused/pallas_call | solution.py:603
  61.4 2.1 %last.1 = (f32[32,16,512]{2,1,0:T(8,128)}, f32[32,32]{1,0:T(8,128)}) custom-call(f32[32,16,512]{2,1,0:T(8,128)} %get-tuple-element.4.raw_ref, f32[8,128]{1,0:T(8,128)} %get-tuple-element.5.sums_hbm), custom_call_target="tpu_custom_call" | custom-call | tf_op jit(solution)/shard_map/last/pallas_call | solution.py:664

commit v7 on v6

--- a/solution.py
+++ b/solution.py
@@ -24,7 +24,7 @@
 VMEM_LIMIT = 60 * 1024 * 1024
 
 MOVES = ((0, 0), (0, 1), (3, 0), (1, 0), (1, 1), (3, 1), (2, 0), (2, 1))
-WAVES = ((1, 3, 2), (4, 6), (5,), (7,))
+WAVES = ((1, 3, 2), (4, 6, 5), (7,), ())
 ROUTES = ((0, 1), (2, 4), (3, 5), (6, 7))
 
 

time: 63.7 us -> 62.7 us (0.984)
  Pallas kernels: 62.9 us -> 62 us
    pallas_call x1, Pallas kernels: 60.8 us -> 59.8 us  [fused(): pl.pallas_call(fused_kernel, out_shape=(jax.ShapeDtypeStruct((CAMS, 16, 5...]
where the time goes in v7:
time: 62.7 us; the launch traced here: 62.6 us
  Pallas kernels  62 us (99%)
  between operations  0.64 us (1%)
    pallas_call x1, Pallas kernels, fused(): pl.pallas_call(fused_kernel, out_shape=(jax.ShapeDtypeStruct((CAMS, 16, 5...  59.8 us
    pallas_call x1, Pallas kernels, last(): pl.pallas_call(last_kernel, out_shape=(jax.ShapeDtypeStruct((CAMS, 16, 51...  2.14 us

profile of v7, /device:TPU:1, one launch (start us, length us, event | category | flops | bytes accessed | tf_op | source)
XLA Modules:
  0.0 62.6 jit_solution(2524076392761126973)
XLA Ops:
  0.6 59.8 %fused.1 = (f32[32,16,512]{2,1,0:T(8,128)}, f32[8,128]{1,0:T(8,128)}) custom-call(bf16[16,16,4096]{2,1,0:T(8,128)(2,1)} %photo_hbm.1, s32[16]{0:T(128)} %cid_ref.1, bf16[256,256]{1,0:T(8,128)(2,1)} %constant.16.clone.rest_0_, bf16[8,256,128]{2,1,0:T(8,128)(2,1)} %constant.17.clone.rest_1_, bf16[128,512]{1,0:T(8,128)(2,1)} %constant.18.clone.rest_2_, ...), custom_call_target="tpu_custom_call" | custom-call | tf_op jit(solution)/shard_map/fused/pallas_call | solution.py:603
  60.5 2.1 %last.1 = (f32[32,16,512]{2,1,0:T(8,128)}, f32[32,32]{1,0:T(8,128)}) custom-call(f32[32,16,512]{2,1,0:T(8,128)} %get-tuple-element.4.raw_ref, f32[8,128]{1,0:T(8,128)} %get-tuple-element.5.sums_hbm), custom_call_target="tpu_custom_call" | custom-call | tf_op jit(solution)/shard_map/last/pallas_call | solution.py:664

commit v8 on v7

--- a/solution.py
+++ b/solution.py
@@ -107,7 +107,7 @@
             sq_ref[b, n] = band * band
         return 0
 
-    lax.fori_loop(0, rows, squares, 0, unroll=2)
+    lax.fori_loop(0, rows, squares, 0, unroll=True)
     x = jnp.concatenate([e_ref[s, n] for n in (0, 1, 2, 4)])
     one = dot(x, haar_edge_ref[...])
     for n in range(rows):
@@ -131,7 +131,7 @@
                 lhs_ref[r - 1, b, i, :, 256:512] = lo
         return 0
 
-    lax.fori_loop(0, HR, sums, 0)
+    lax.fori_loop(0, HR, sums, 0, unroll=True)
 
     for r in range(4):
         got = dot(lhs_ref[r].reshape(3 * HR * OWN, 512), box_ref[r])
@@ -161,7 +161,7 @@
                 data_ref[2 * j + part, pl.ds(HR * OWN + at, OWN), :] = lo
         return 0
 
-    lax.fori_loop(0, HR, residual, 0)
+    lax.fori_loop(0, HR, residual, 0, unroll=True)
 
     ids = e_ref[s, 3].astype(F32)[0:1, :]
     row = lax.broadcasted_iota(jnp.int32, (256, 128), 0)

time: 62.7 us -> 61 us (0.973)
  Pallas kernels: 62 us -> 60.2 us
    pallas_call x1, Pallas kernels: 59.8 us -> 58 us  [fused(): pl.pallas_call(fused_kernel, out_shape=(jax.ShapeDtypeStruct((CAMS, 16, 5...]
where the time goes in v8:
time: 61 us; the launch traced here: 60.8 us
  Pallas kernels  60.2 us (99%)
  between operations  0.64 us (1%)
    pallas_call x1, Pallas kernels, fused(): pl.pallas_call(fused_kernel, out_shape=(jax.ShapeDtypeStruct((CAMS, 16, 5...  58 us
    pallas_call x1, Pallas kernels, last(): pl.pallas_call(last_kernel, out_shape=(jax.ShapeDtypeStruct((CAMS, 16, 51...  2.14 us

profile of v8, /device:TPU:1, one launch (start us, length us, event | category | flops | bytes accessed | tf_op | source)
XLA Modules:
  0.0 60.8 jit_solution(15974855546536084394)
XLA Ops:
  0.6 58.0 %fused.1 = (f32[32,16,512]{2,1,0:T(8,128)}, f32[8,128]{1,0:T(8,128)}) custom-call(bf16[16,16,4096]{2,1,0:T(8,128)(2,1)} %photo_hbm.1, s32[16]{0:T(128)} %cid_ref.1, bf16[256,256]{1,0:T(8,128)(2,1)} %constant.16.clone.rest_0_, bf16[8,256,128]{2,1,0:T(8,128)(2,1)} %constant.17.clone.rest_1_, bf16[128,512]{1,0:T(8,128)(2,1)} %constant.18.clone.rest_2_, ...), custom_call_target="tpu_custom_call" | custom-call | tf_op jit(solution)/shard_map/fused/pallas_call | solution.py:603
  58.7 2.1 %last.1 = (f32[32,16,512]{2,1,0:T(8,128)}, f32[32,32]{1,0:T(8,128)}) custom-call(f32[32,16,512]{2,1,0:T(8,128)} %get-tuple-element.4.raw_ref, f32[8,128]{1,0:T(8,128)} %get-tuple-element.5.sums_hbm), custom_call_target="tpu_custom_call" | custom-call | tf_op jit(solution)/shard_map/last/pallas_call | solution.py:664
